TPU v7x, 256 devices: a whole 4x4x8 slice. The times are simulated.
256 devices in a mesh: img: 4 (over y), seq: 64 (over z, x, core).
Axes of the slice: x: 4, y: 4, z: 8, core: 2. Of those that a mesh axis runs over, the one named last changes fastest.
Arguments:
- query_proj: bfloat16 [4, 8192, 1280], P('img', 'seq'), may hold values from -6 to 6
- key_proj: bfloat16 [4, 8192, 1280], P('img', 'seq'), may hold values from -6 to 6
- value_proj: bfloat16 [4, 8192, 1280], P('img', 'seq'), may hold values from -12 to 12
- merge_cells: int32 [4, 2048, 4], P('img', 'seq'), may hold values from 0 to 8191, as said below
- unmerge: int32 [4, 8192], P('img', 'seq'), may hold values from 0 to 2047, as said below
- grad_out: bfloat16 [4, 8192, 1280], P('img', 'seq'), may hold values from -9 to 9
- query_gain: float32 [64], replicated, may hold values from 1 to 2.5
- key_gain: float32 [64], replicated, may hold values from 1 to 2.5
Outputs:
- attended: bfloat16 [4, 8192, 1280], P('img', 'seq')
- grad_query: bfloat16 [4, 8192, 1280], P('img', 'seq')
- grad_key: bfloat16 [4, 8192, 1280], P('img', 'seq')
- grad_value: bfloat16 [4, 8192, 1280], P('img', 'seq')
- grad_query_gain: float32 [64], replicated
- grad_key_gain: float32 [64], replicated
Inputs may be any that keep to these rules, and one draw needn't show every extreme that they name: `merge_cells`: row c of an image lists, in some order, the four tokens of one 2x2 cell: columns j and j + 1 (modulo 64) of image rows 2 i and 2 i + 1, where token r * 64 + s stands at row r and column s and j has one parity within each pair of rows; every token lies in exactly one cell; cell c and its four tokens are held by the same seq index. `unmerge`: entry t is the row of merge_cells of the same image that lists token t.
All inputs are finite; a program needn't handle non-finite values.
Results may differ from a plain program's by a relative error of at most 0.012.
Values may be sent and summed in bfloat16 or wider, within the bound.
A program may use at most 128 MiB of HBM per device.

v0:
```python
import math

import jax
import jax.numpy as jnp
from jax import lax
from jax.sharding import PartitionSpec as P

EPSILON = 1e-06
PRECISE = lax.Precision.HIGHEST


def normalize(inputs, gain_row):
    row_scale = lax.rsqrt(jnp.mean(inputs * inputs, axis=-1, keepdims=True) + EPSILON)
    unit_vals = inputs * row_scale
    return (unit_vals, row_scale, unit_vals * gain_row)


def norm_back(grad_normed, unit_vals, row_scale, gain_row):
    grad_unit = grad_normed * gain_row
    mean_inner = jnp.mean(grad_unit * unit_vals, axis=-1, keepdims=True)
    return row_scale * (grad_unit - unit_vals * mean_inner)


def attention_pass(queries, upstream, keys_all, values_all):
    tok_rows, group_heads, head_dim = queries.shape
    group_lanes = group_heads * head_dim
    cell_count = keys_all.shape[0]
    block_rows = math.gcd(cell_count, 512)
    block_count = cell_count // block_rows
    key_blocks = keys_all.reshape(block_count, block_rows, group_lanes)
    value_blocks = values_all.reshape(block_count, block_rows, group_lanes)

    def scores_of(key_rows):
        return (
            jnp.einsum(
                "thd,khd->thk",
                queries,
                key_rows.reshape(-1, group_heads, head_dim),
                preferred_element_type=jnp.float32,
            )
            * 0.125
        )

    def forward_step(running, pieces):
        row_total, weighted = running
        key_rows, value_rows = pieces
        exp_scores = jnp.exp(scores_of(key_rows))
        row_total = row_total + jnp.sum(exp_scores, axis=-1)
        weighted = weighted + jnp.einsum(
            "thk,khd->thd",
            exp_scores.astype(jnp.bfloat16),
            value_rows.reshape(-1, group_heads, head_dim),
            preferred_element_type=jnp.float32,
        )
        return ((row_total, weighted), None)

    initial = (
        jnp.zeros((tok_rows, group_heads), jnp.float32),
        jnp.zeros((tok_rows, group_heads, head_dim), jnp.float32),
    )
    (row_total, weighted), unused = lax.scan(forward_step, initial, (key_blocks, value_blocks))
    attended = (weighted / row_total[:, :, None]).astype(jnp.bfloat16)
    row_inner = jnp.sum(upstream.astype(jnp.float32) * attended.astype(jnp.float32), axis=-1)

    def local_grads(key_rows, value_rows):
        attention = jnp.exp(scores_of(key_rows)) / row_total[:, :, None]
        grad_weights = jnp.einsum(
            "thd,khd->thk",
            upstream,
            value_rows.reshape(-1, group_heads, head_dim),
            preferred_element_type=jnp.float32,
        )
        grad_scores = (attention * (grad_weights - row_inner[:, :, None])).astype(jnp.bfloat16)
        return (attention.astype(jnp.bfloat16), grad_scores)

    def key_terms(key_rows, attention_bf, grad_scores):
        row_count = key_rows.shape[0]
        grad_keys = (
            jnp.einsum("thk,thd->khd", grad_scores, queries, preferred_element_type=jnp.float32)
            * 0.125
        )
        grad_values = jnp.einsum(
            "thk,thd->khd", attention_bf, upstream, preferred_element_type=jnp.float32
        )
        return jnp.concatenate(
            [
                grad_keys.reshape(row_count, group_lanes),
                grad_values.reshape(row_count, group_lanes),
            ],
            axis=1,
        )

    def query_term(key_rows, grad_scores):
        return (
            jnp.einsum(
                "thk,khd->thd",
                grad_scores,
                key_rows.reshape(-1, group_heads, head_dim),
                preferred_element_type=jnp.float32,
            )
            * 0.125
        )

    query_zero = jnp.zeros((tok_rows, group_heads, head_dim), jnp.float32)

    def backward_step(running, pieces):
        key_rows, value_rows = pieces
        attention_bf, grad_scores = local_grads(key_rows, value_rows)
        return (
            running + query_term(key_rows, grad_scores),
            key_terms(key_rows, attention_bf, grad_scores),
        )

    grad_q_group, term_blocks = lax.scan(backward_step, query_zero, (key_blocks, value_blocks))
    return (attended, grad_q_group, term_blocks.reshape(cell_count, 2 * group_lanes), None)


def local(query_proj, key_proj, value_proj, merge_cells, unmerge, grad_out, query_gain, key_gain):
    tok_dev = query_proj.shape[1]
    total_lanes = query_proj.shape[2]
    head_dim = query_gain.shape[0]
    head_count = total_lanes // head_dim
    cells_dev = merge_cells.shape[1]
    seq_index = lax.axis_index("seq")
    q_unit, q_scale, q_normed = normalize(
        query_proj[0].astype(jnp.float32).reshape(tok_dev, head_count, head_dim), query_gain
    )
    q_bf = q_normed.reshape(tok_dev, total_lanes).astype(jnp.bfloat16)
    k_unit, k_scale, k_normed = normalize(
        key_proj[0].astype(jnp.float32).reshape(tok_dev, head_count, head_dim), key_gain
    )
    tok_ids = seq_index * tok_dev + jnp.arange(tok_dev, dtype=jnp.int32)
    member = jnp.sum(
        (merge_cells[0][:, :, None] == tok_ids[None, None, :]).astype(jnp.float32), axis=1
    )
    k_merged = (
        jnp.dot(member, k_normed.reshape(tok_dev, total_lanes), precision=PRECISE) * 0.25
    ).astype(jnp.bfloat16)
    v_merged = (
        jnp.dot(member.astype(jnp.bfloat16), value_proj[0], preferred_element_type=jnp.float32)
        * 0.25
    ).astype(jnp.bfloat16)
    group_lanes = 256
    group_heads = group_lanes // head_dim
    out_parts, query_parts, key_parts, value_parts = ([], [], [], [])
    for group_index in range(total_lanes // group_lanes):
        lane_start = group_index * group_lanes
        queries = q_bf[:, lane_start : lane_start + group_lanes].reshape(
            tok_dev, group_heads, head_dim
        )
        upstream = grad_out[0][:, lane_start : lane_start + group_lanes].reshape(
            tok_dev, group_heads, head_dim
        )
        keys_all, values_all = (
            lax.all_gather(
                k_merged[:, lane_start : lane_start + group_lanes], "seq", axis=0, tiled=True
            ),
            lax.all_gather(
                v_merged[:, lane_start : lane_start + group_lanes], "seq", axis=0, tiled=True
            ),
        )
        attended, grad_q_group, term_rows, unused = attention_pass(
            queries, upstream, keys_all, values_all
        )
        reduced = lax.psum_scatter(term_rows, "seq", scatter_dimension=0, tiled=True)
        out_parts.append(attended.reshape(tok_dev, group_lanes))
        query_parts.append(grad_q_group.reshape(tok_dev, group_lanes))
        key_parts.append(reduced[:, :group_lanes])
        value_parts.append(reduced[:, group_lanes:])
    attended_all = jnp.concatenate(out_parts, axis=1)
    grad_q_normed = jnp.concatenate(query_parts, axis=1).reshape(tok_dev, head_count, head_dim)
    grad_merged_k = jnp.concatenate(key_parts, axis=1)
    grad_merged_v = jnp.concatenate(value_parts, axis=1)
    cell_ids = seq_index * cells_dev + jnp.arange(cells_dev, dtype=jnp.int32)
    unmerge_table = (unmerge[0][:, None] == cell_ids[None, :]).astype(jnp.float32)
    grad_k_normed = (jnp.dot(unmerge_table, grad_merged_k, precision=PRECISE) * 0.25).reshape(
        tok_dev, head_count, head_dim
    )
    grad_value = (jnp.dot(unmerge_table, grad_merged_v, precision=PRECISE) * 0.25).astype(
        jnp.bfloat16
    )
    gain_terms = (
        jnp.sum(grad_q_normed * q_unit, axis=(0, 1)),
        jnp.sum(grad_k_normed * k_unit, axis=(0, 1)),
    )
    grad_query_gain, grad_key_gain = lax.psum((gain_terms[0], gain_terms[1]), ("img", "seq"))
    grad_query = (
        norm_back(grad_q_normed, q_unit, q_scale, query_gain)
        .reshape(tok_dev, total_lanes)
        .astype(jnp.bfloat16)
    )
    grad_key = (
        norm_back(grad_k_normed, k_unit, k_scale, key_gain)
        .reshape(tok_dev, total_lanes)
        .astype(jnp.bfloat16)
    )
    return (
        attended_all[None],
        grad_query[None],
        grad_key[None],
        grad_value[None],
        grad_query_gain,
        grad_key_gain,
    )


def solution(mesh):
    placed = (
        P("img", "seq", None),
        P("img", "seq", None),
        P("img", "seq", None),
        P("img", "seq", None),
        P("img", "seq"),
        P("img", "seq", None),
        P(),
        P(),
    )
    return jax.shard_map(
        local,
        mesh=mesh,
        in_specs=placed,
        out_specs=(
            P("img", "seq", None),
            P("img", "seq", None),
            P("img", "seq", None),
            P("img", "seq", None),
            P(),
            P(),
        ),
        check_vma=False,
    )
```

profile of v0, /device:TPU:1, one launch (start us, length us, event | category | flops | bytes accessed | tf_op | source)
XLA Modules:
  0.0 1611.3 jit_solution(1745395088641482915)
XLA Ops:
  22.7 71.7 %all-gather.11.cloned.1.call-done = bf16[2048,256]{1,0:T(8,128)(2,1)} async-done(((bf16[32,256]{1,0:T(8,128)(2,1)}), bf16[2048,256]{1,0:T(8,128)(2,1)}) %all-gather.11.cloned.1.call-update) | async-done | bytes 1048592 | tf_op jit(solution)/shard_map/all_gather | solution.py:155
  96.7 75.1 %all-gather.13.cloned.1.call-done = bf16[2048,256]{1,0:T(8,128)(2,1)} async-done(((bf16[32,256]{1,0:T(8,128)(2,1)}), bf16[2048,256]{1,0:T(8,128)(2,1)}) %all-gather.13.cloned.1.call-update) | async-done | bytes 1048592 | tf_op jit(solution)/shard_map/all_gather | solution.py:158
  174.1 14.6 while.130
  192.6 28.4 %while.135 = (s32[]{:T(128)}, f32[128,4,64]{0,2,1:T(8,128)}, f32[4,512,512]{2,1,0:T(8,128)}, bf16[4,512,256]{1,2,0:T(8,128)(2,1)}, bf16[128,4,64]{0,2,1:T(8,128)...) while((s32[]{:T(128)}, f32[128,4,64]{0,2,1:T(8,128)}, ...), condition=%wide.region_20.21_spmd.clone, body=%wide.region_19.20_spmd.clone.sunk | while | flops 169836544 | bytes 14422651 | solution.py:114
  221.0 28.1 %all-gather.15.cloned.1.call-done = bf16[2048,256]{1,0:T(8,128)(2,1)} async-done(((bf16[32,256]{1,0:T(8,128)(2,1)}), bf16[2048,256]{1,0:T(8,128)(2,1)}) %all-gather.15.cloned.1.call-update) | async-done | bytes 1048592 | tf_op jit(solution)/shard_map/all_gather | solution.py:155
  251.4 74.9 %all-gather.17.cloned.1.call-done = bf16[2048,256]{1,0:T(8,128)(2,1)} async-done(((bf16[32,256]{1,0:T(8,128)(2,1)}), bf16[2048,256]{1,0:T(8,128)(2,1)}) %all-gather.17.cloned.1.call-update) | async-done | bytes 1048592 | tf_op jit(solution)/shard_map/all_gather | solution.py:158
  338.9 64.5 %all-gather.19.cloned.1.call-done = bf16[2048,256]{1,0:T(8,128)(2,1)} async-done(((bf16[32,256]{1,0:T(8,128)(2,1)}), bf16[2048,256]{1,0:T(8,128)(2,1)}) %all-gather.19.cloned.1.call-update) | async-done | bytes 1048592 | tf_op jit(solution)/shard_map/all_gather | solution.py:155
  405.7 74.9 %all-gather.21.cloned.1.call-done = bf16[2048,256]{1,0:T(8,128)(2,1)} async-done(((bf16[32,256]{1,0:T(8,128)(2,1)}), bf16[2048,256]{1,0:T(8,128)(2,1)}) %all-gather.21.cloned.1.call-update) | async-done | bytes 1048592 | tf_op jit(solution)/shard_map/all_gather | solution.py:158
  482.9 10.4 while.132
  493.3 64.7 %all-gather.23.cloned.1.call-done = bf16[2048,256]{1,0:T(8,128)(2,1)} async-done(((bf16[32,256]{1,0:T(8,128)(2,1)}), bf16[2048,256]{1,0:T(8,128)(2,1)}) %all-gather.23.cloned.1.call-update) | async-done | bytes 1048592 | tf_op jit(solution)/shard_map/all_gather | solution.py:155
  560.2 75.0 %all-gather.25.cloned.1.call-done = bf16[2048,256]{1,0:T(8,128)(2,1)} async-done(((bf16[32,256]{1,0:T(8,128)(2,1)}), bf16[2048,256]{1,0:T(8,128)(2,1)}) %all-gather.25.cloned.1.call-update) | async-done | bytes 1048592 | tf_op jit(solution)/shard_map/all_gather | solution.py:158
  637.6 75.1 %all-gather.27.cloned.1.call-done = bf16[2048,256]{1,0:T(8,128)(2,1)} async-done(((bf16[32,256]{1,0:T(8,128)(2,1)}), bf16[2048,256]{1,0:T(8,128)(2,1)}) %all-gather.27.cloned.1.call-update) | async-done | bytes 1048592 | tf_op jit(solution)/shard_map/all_gather | solution.py:155
  714.9 12.2 while.133
  727.4 62.4 %all-gather.29.cloned.1.call-done = bf16[2048,256]{1,0:T(8,128)(2,1)} async-done(((bf16[32,256]{1,0:T(8,128)(2,1)}), bf16[2048,256]{1,0:T(8,128)(2,1)}) %all-gather.29.cloned.1.call-update) | async-done | bytes 1048592 | tf_op jit(solution)/shard_map/all_gather | solution.py:158
  802.3 28.5 %while.136 = (s32[]{:T(128)}, f32[128,4,64]{0,2,1:T(8,128)}, f32[4,512,512]{2,1,0:T(8,128)}, bf16[4,512,256]{1,2,0:T(8,128)(2,1)}, bf16[128,4,64]{0,2,1:T(8,128)...) while((s32[]{:T(128)}, f32[128,4,64]{0,2,1:T(8,128)}, ...), condition=%wide.region_23.24_spmd.clone, body=%wide.region_22.23_spmd.clone.sunk | while | flops 169836544 | bytes 14422651 | solution.py:114
  835.0 23.3 %while.137 = (s32[]{:T(128)}, f32[128,4,64]{0,2,1:T(8,128)S(1)}, f32[4,512,512]{2,1,0:T(8,128)}, bf16[4,512,256]{1,2,0:T(8,128)(2,1)}, bf16[128,4,64]{0,2,1:T(8,...) while((s32[]{:T(128)}, f32[128,4,64]{0,2,1:T(8,128)S(1)}, ...), condition=%wide.region_26.27_spmd.clone, body=%wide.region_25.26_spmd.clone.sunk | while | flops 169836544 | bytes 14422651 | solution.py:114
  862.4 16.5 %while.138 = (s32[]{:T(128)}, f32[128,4,64]{0,2,1:T(8,128)S(1)}, f32[4,512,512]{2,1,0:T(8,128)}, bf16[4,512,256]{1,2,0:T(8,128)(2,1)}, bf16[128,4,64]{0,2,1:T(8,...) while((s32[]{:T(128)}, f32[128,4,64]{0,2,1:T(8,128)S(1)}, ...), condition=%wide.region_29.30_spmd.clone, body=%wide.region_28.29_spmd.clone.sunk | while | flops 169836544 | bytes 14422651 | solution.py:114
  883.0 16.5 %while.139 = (s32[]{:T(128)}, f32[128,4,64]{0,2,1:T(8,128)S(1)}, f32[4,512,512]{2,1,0:T(8,128)}, bf16[4,512,256]{1,2,0:T(8,128)(2,1)}, bf16[128,4,64]{0,2,1:T(8,...) while((s32[]{:T(128)}, f32[128,4,64]{0,2,1:T(8,128)S(1)}, ...), condition=%wide.region_32.33_spmd.clone, body=%wide.region_31.32_spmd.clone.sunk | while | flops 169836544 | bytes 14422651 | solution.py:114
  905.2 25.4 %reduce-scatter.6.cloned.1.call-done = f32[32,512]{1,0:T(8,128)} async-done(((f32[2048,512]{1,0:T(8,128)}), f32[32,512]{1,0:T(8,128)}) %reduce-scatter.6.cloned.1.call-update) | async-done | bytes 65552 | tf_op jit(solution)/shard_map/reduce_scatter | solution.py:165
  931.3 146.0 %reduce-scatter.8.cloned.1.call-done = f32[32,512]{1,0:T(8,128)} async-done(((f32[2048,512]{1,0:T(8,128)}), f32[32,512]{1,0:T(8,128)}) %reduce-scatter.8.cloned.1.call-update) | async-done | bytes 65552 | tf_op jit(solution)/shard_map/reduce_scatter | solution.py:165
  1078.1 146.1 %reduce-scatter.10.cloned.1.call-done = f32[32,512]{1,0:T(8,128)} async-done(((f32[2048,512]{1,0:T(8,128)}), f32[32,512]{1,0:T(8,128)}) %reduce-scatter.10.cloned.1.call-update) | async-done | bytes 65552 | tf_op jit(solution)/shard_map/reduce_scatter | solution.py:165
  1225.0 145.9 %reduce-scatter.12.cloned.1.call-done = f32[32,512]{1,0:T(8,128)} async-done(((f32[2048,512]{1,0:T(8,128)}), f32[32,512]{1,0:T(8,128)}) %reduce-scatter.12.cloned.1.call-update) | async-done | bytes 65552 | tf_op jit(solution)/shard_map/reduce_scatter | solution.py:165
  1371.7 145.9 %reduce-scatter.14.cloned.1.call-done = f32[32,512]{1,0:T(8,128)} async-done(((f32[2048,512]{1,0:T(8,128)}), f32[32,512]{1,0:T(8,128)}) %reduce-scatter.14.cloned.1.call-update) | async-done | bytes 65552 | tf_op jit(solution)/shard_map/reduce_scatter | solution.py:165
  1525.2 79.5 %all-reduce = (f32[64]{0:T(128)}, f32[64]{0:T(128)}) all-reduce(f32[64]{0:T(128)S(1)} %reduce_sum.179, f32[64]{0:T(128)S(1)} %reduce_sum.182), channel_id=1, replica_groups=mesh['img'=4,'seq'=64] {'img','seq'}, use_global_device_ids=true, to_apply=%region_42.43 | all-reduce | flops 128 | bytes 1024 | tf_op jit(solution)/shard_map/psum | solution.py:186
  (473 shorter events, 257.0 us)
Async XLA Ops:
  7.2 87.2 %all-gather.11.cloned.1.call-start = ((), (), s32[]{:S(2)}) async-start(), calls=%async_computation.5 | async-start | bytes 1064960 | tf_op jit(solution)/shard_map/all_gather | solution.py:155
  13.4 158.4 %all-gather.13.cloned.1.call-start = ((), (), s32[]{:S(2)}) async-start(), calls=%async_computation.6 | async-start | bytes 1064960 | tf_op jit(solution)/shard_map/all_gather | solution.py:158
  14.3 234.8 %all-gather.15.cloned.1.call-start = ((), (), s32[]{:S(2)}) async-start(), calls=%async_computation.7 | async-start | bytes 1064960 | tf_op jit(solution)/shard_map/all_gather | solution.py:155
  15.0 311.3 %all-gather.17.cloned.1.call-start = ((), (), s32[]{:S(2)}) async-start(), calls=%async_computation.8 | async-start | bytes 1064960 | tf_op jit(solution)/shard_map/all_gather | solution.py:158
  15.6 387.9 %all-gather.19.cloned.1.call-start = ((), (), s32[]{:S(2)}) async-start(), calls=%async_computation.9 | async-start | bytes 1064960 | tf_op jit(solution)/shard_map/all_gather | solution.py:155
  16.2 464.5 %all-gather.21.cloned.1.call-start = ((), (), s32[]{:S(2)}) async-start(), calls=%async_computation.10 | async-start | bytes 1064960 | tf_op jit(solution)/shard_map/all_gather | solution.py:158
  16.8 541.2 %all-gather.23.cloned.1.call-start = ((), (), s32[]{:S(2)}) async-start(), calls=%async_computation.11 | async-start | bytes 1064960 | tf_op jit(solution)/shard_map/all_gather | solution.py:155
  17.5 617.8 %all-gather.25.cloned.1.call-start = ((), (), s32[]{:S(2)}) async-start(), calls=%async_computation.12 | async-start | bytes 1064960 | tf_op jit(solution)/shard_map/all_gather | solution.py:158
  18.3 694.4 %all-gather.27.cloned.1.call-start = ((), (), s32[]{:S(2)}) async-start(), calls=%async_computation.13 | async-start | bytes 1064960 | tf_op jit(solution)/shard_map/all_gather | solution.py:155
  19.0 770.8 %all-gather.29.cloned.1.call-start = ((), (), s32[]{:S(2)}) async-start(), calls=%async_computation.14 | async-start | bytes 1064960 | tf_op jit(solution)/shard_map/all_gather | solution.py:158
  19.6 911.0 %reduce-scatter.6.cloned.1.call-start = ((), (), s32[]{:S(2)}) async-start(), calls=%async_computation.15 | async-start | bytes 4259840 | tf_op jit(solution)/shard_map/reduce_scatter | solution.py:165
  338.9 144.0 %copy-start.13 = (f32[128,4,64]{0,2,1:T(8,128)S(1)}, f32[128,4,64]{0,2,1:T(8,128)}, u32[]{:S(2)}) copy-start(f32[128,4,64]{0,2,1:T(8,128)} %custom-call.5) | copy-start | bytes 393220
  493.3 221.6 %copy-start.14 = (f32[128,4,64]{0,2,1:T(8,128)}, f32[128,4,64]{0,2,1:T(8,128)S(1)}, u32[]{:S(2)}) copy-start(f32[128,4,64]{0,2,1:T(8,128)S(1)} %get-tuple-element.415) | copy-start | bytes 393220
  493.3 221.6 %copy-start.20 = (bf16[128,256]{0,1:T(8,128)(2,1)S(1)}, bf16[128,256]{0,1:T(8,128)(2,1)}, u32[]{:S(2)}) copy-start(bf16[128,256]{0,1:T(8,128)(2,1)} %get-tuple-element.1122) | copy-start | bytes 196612
  727.2 350.1 %reduce-scatter.8.cloned.1.call-start = ((), (), s32[]{:S(2)}) async-start(), calls=%async_computation.16 | async-start | bytes 4259840 | tf_op jit(solution)/shard_map/reduce_scatter | solution.py:165
  830.8 393.4 %reduce-scatter.10.cloned.1.call-start = ((), (), s32[]{:S(2)}) async-start(), calls=%async_computation.17 | async-start | bytes 4259840 | tf_op jit(solution)/shard_map/reduce_scatter | solution.py:165
  858.3 512.7 %reduce-scatter.12.cloned.1.call-start = ((), (), s32[]{:S(2)}) async-start(), calls=%async_computation.18 | async-start | bytes 4259840 | tf_op jit(solution)/shard_map/reduce_scatter | solution.py:165
  878.9 638.7 %reduce-scatter.14.cloned.1.call-start = ((), (), s32[]{:S(2)}) async-start(), calls=%async_computation.19 | async-start | bytes 4259840 | tf_op jit(solution)/shard_map/reduce_scatter | solution.py:165
  899.7 619.4 %copy-start.41 = (s32[1,128]{1,0:T(1,128)S(1)}, s32[1,128]{1,0:T(1,128)}, u32[]{:S(2)}) copy-start(s32[1,128]{1,0:T(1,128)} %param.32) | copy-start | bytes 1540
  900.6 620.9 %copy-start.5 = (f32[1,128,1280]{1,2,0:T(8,128)S(1)}, f32[1,128,1280]{1,2,0:T(8,128)}, u32[]{:S(2)}) copy-start(f32[1,128,1280]{1,2,0:T(8,128)} %copy-done.4) | copy-start | bytes 1966084
  900.6 620.8 %copy-start.32 = (f32[128,20]{0,1:T(8,128)S(1)}, f32[128,20]{0,1:T(8,128)}, u32[]{:S(2)}) copy-start(f32[128,20]{0,1:T(8,128)} %copy-done.31) | copy-start | bytes 30724
  900.6 620.8 %copy-start.40 = (f32[64]{0:T(128)S(1)}, f32[64]{0:T(128)}, u32[]{:S(2)}) copy-start(f32[64]{0:T(128)} %param.35) | copy-start | bytes 772
  902.4 620.6 %copy-start.3 = (f32[128,1280]{1,0:T(8,128)S(1)}, f32[128,1280]{1,0:T(8,128)}, u32[]{:S(2)}) copy-start(f32[128,1280]{1,0:T(8,128)} %copy-done.2) | copy-start | bytes 1966084
  902.4 620.6 %copy-start.18 = (bf16[1,128,1280]{2,1,0:T(8,128)(2,1)S(1)}, bf16[1,128,1280]{2,1,0:T(8,128)(2,1)}, u32[]{:S(2)}) copy-start(bf16[1,128,1280]{2,1,0:T(8,128)(2,1)} %param.29) | copy-start | bytes 983044
  (34 other events, 549.6 us)
Sparse Core Ops, SparseCore 0:
  13.5 80.9 all-gather.10
  97.2 74.5 all-gather.12
  174.5 74.5 all-gather.14
  251.7 74.5 all-gather.16
  328.9 74.5 all-gather.18
  406.1 74.5 all-gather.20
  483.4 74.5 all-gather.22
  560.7 74.5 all-gather.24
  638.1 74.5 all-gather.26
  715.2 74.5 all-gather.28
  793.9 136.5 reduce-scatter.5
  934.5 142.7 reduce-scatter.7
  1081.4 142.7 reduce-scatter.9
  1228.2 142.6 reduce-scatter.11
  1374.9 142.6 reduce-scatter.13
where the time goes:
time: 1620 us; the launch traced here: 1610 us
  waiting for transfers between devices  1280 us (79%)
  local copies, waits for them, and re-layouts  124 us (8%)
  matrix products  93.7 us (6%)
  blocking collectives  79.5 us (5%)
  other arithmetic  16.3 us (1%)
    reduce_scatter x5, waiting for transfers between devices, local(): lax.psum_scatter(term_rows, 'seq', scatter_dimension=0, tiled=True)  609 us
    all_gather x5, waiting for transfers between devices, local(): lax.all_gather(v_merged[:, lane_start:lane_start + group_lanes], 'seq', a...  362 us
    all_gather x5, waiting for transfers between devices, local(): lax.all_gather(k_merged[:, lane_start:lane_start + group_lanes], 'seq', a...  304 us
    psum x1, blocking collectives, local(): lax.psum((gain_terms[0], gain_terms[1]), ('img', 'seq'))  79.5 us
    dynamic_slice x40, local copies, waits for them, and re-layouts, attention_pass(): lax.scan(forward_step, initial, (key_blocks, value_blocks))  42.7 us
    dot_general x40, matrix products, scores_of(): jnp.einsum('thd,khd->thk', queries, key_rows.reshape(-1, group_heads, hea...  35.5 us
    unnamed x111, local copies, waits for them, and re-layouts  32.6 us
  transfers between devices with their start and end apart: 15, of which 15 were waited for; matrix products, arithmetic and copies ran while one was open for 14% of the time, Pallas kernels for 0%

commit v1 on v0

v1 whole, which is shorter than its diff:
```python
import functools

import jax
import jax.numpy as jnp
from jax import lax
from jax.experimental import pallas as pl
from jax.experimental.pallas import tpu as pltpu
from jax.sharding import PartitionSpec as P

BF = jnp.bfloat16
F32 = jnp.float32
EPSILON = 1e-06
NZ, NX = 8, 4
HEADS = ((0, 1, 0, 0), (0, 1, 64, 64), (2, 3, 0, 0), (2, 3, 64, 64), (4, 4, 0, 64))


def dot(a, b):
    return jnp.dot(a, b, preferred_element_type=F32)


def dot_t(a, b):
    return lax.dot_general(a, b, (((1,), (1,)), ((), ())), preferred_element_type=F32)


def dot_l(a, b):
    return lax.dot_general(a, b, (((0,), (0,)), ((), ())), preferred_element_type=F32)


def split(value):
    high = value.astype(BF)
    return high, (value - high.astype(F32)).astype(BF)


def kernel(
    ny,
    q_in,
    k_in,
    v_in,
    merge_in,
    unmerge_in,
    g_in,
    q_gain,
    k_gain,
    att_out,
    gq_out,
    gk_out,
    gv_out,
    gain_out,
    q_unit,
    q_scale,
    k_unit,
    k_scale,
    kv_stage,
    qg_stage,
    kv,
    qg,
    qm,
    gm,
    q_t,
    g_t,
    es,
    acc,
    gq_acc,
    g_all,
    core_send,
    core_recv,
    up_send,
    up_recv,
    dn_send,
    dn_recv,
    out_stage,
    out_recv,
    cell_stage,
    cell_recv,
    gain_own,
    gain_core,
    gain_x,
    gain_y,
    gain_z,
    sem_xs,
    sem_xr,
    sem_us,
    sem_ur,
    sem_ds,
    sem_dr,
    sem_ps,
    sem_pr,
    sem_cs,
    sem_cr,
    sem_rus,
    sem_rur,
    sem_rds,
    sem_rdr,
    sem_gs,
    sem_gr,
):
    img = lax.axis_index("img")
    seq = lax.axis_index("seq")
    core = seq % 2
    x = (seq // 2) % NX
    z = seq // (2 * NX)
    other = 1 - core

    def at(zz, xx, cc):
        return (img, (zz * NX + xx) * 2 + cc)

    up = at((z + 1) % NZ, x, core)
    down = at((z + NZ - 1) % NZ, x, core)
    partner = at(z, x, other)
    x_peers = [at(z, (x + d) % NX, core) for d in range(1, NX)]
    z_peers = [at((z + d) % NZ, x, core) for d in range(1, NZ)]
    y_peers = [((img + d) % ny, seq) for d in range(1, ny)]
    barrier = pltpu.get_barrier_semaphore()
    greeted = [partner] + x_peers + z_peers + y_peers
    for device in greeted:
        pl.semaphore_signal(barrier, inc=1, device_id=device, device_id_type=pl.DeviceIdType.MESH)

    def remote(src, dst, send_sem, recv_sem, device):
        return pltpu.make_async_remote_copy(
            src_ref=src,
            dst_ref=dst,
            send_sem=send_sem,
            recv_sem=recv_sem,
            device_id=device,
            device_id_type=pl.DeviceIdType.MESH,
        )

    lane = lax.broadcasted_iota(jnp.int32, (1, 128), 1)
    low = lane < 64
    head_sum = (
        (lax.broadcasted_iota(jnp.int32, (128, 128), 0) < 64)
        == (lax.broadcasted_iota(jnp.int32, (128, 128), 1) < 64)
    ).astype(F32).astype(BF)

    def head_mean(value):
        high, rest = split(value)
        return (dot(high, head_sum) + dot(rest, head_sum)) * (1.0 / 64.0)

    gain_q = jnp.concatenate([q_gain[...], q_gain[...]], axis=1)
    gain_k = jnp.concatenate([k_gain[...], k_gain[...]], axis=1)
    token = seq * 128 + lane
    cells = merge_in[0]
    member = jnp.zeros((32, 128), F32)
    for j in range(4):
        member = member + (cells[:, j : j + 1] == token).astype(F32)
    member = member.astype(BF)

    def pick(first, second, which):
        if which == 0:
            return jnp.where(low, first, pltpu.roll(second, 64, 1)).astype(BF)
        return jnp.where(low, pltpu.roll(first, 64, 1), second).astype(BF)

    for pair in range(10):
        lanes = slice(pair * 128, pair * 128 + 128)
        raw = k_in[0, :, lanes].astype(F32)
        scale = lax.rsqrt(head_mean(raw * raw) + EPSILON)
        unit = raw * scale
        k_unit[:, lanes] = unit
        k_scale[:, lanes] = scale
        high, rest = split(unit * gain_k)
        merged_k = (dot(member, high) + dot(member, rest)) * 0.25
        merged_v = dot(member, v_in[0, :, lanes]) * 0.25
        if pair < 8:
            kv_stage[pair // 2, (pair % 2) * 2] = merged_k.astype(BF)
            kv_stage[pair // 2, (pair % 2) * 2 + 1] = merged_v.astype(BF)
        else:
            for which in range(2):
                kv_stage[(pair - 8) * 2 + which, 4] = pick(merged_k, merged_v, which)
    pl.semaphore_wait(barrier, len(greeted))

    def kv_x(d):
        return remote(
            kv_stage.at[(x + d) % NX],
            kv.at[:, z, core, pl.ds(pl.multiple_of(x * 32, 32), 32), :],
            sem_xs.at[0, d - 1],
            sem_xr.at[0, d - 1],
            x_peers[d - 1],
        )

    def qg_x(d):
        return remote(
            qg_stage.at[(x + d) % NX], qg.at[x], sem_xs.at[1, d - 1], sem_xr.at[1, d - 1], x_peers[d - 1]
        )

    for d in range(1, NX):
        kv_x(d).start()
    kv[:, z, core, pl.ds(pl.multiple_of(x * 32, 32), 32), :] = kv_stage[x]
    for pair in range(10):
        lanes = slice(pair * 128, pair * 128 + 128)
        raw = q_in[0, :, lanes].astype(F32)
        scale = lax.rsqrt(head_mean(raw * raw) + EPSILON)
        unit = raw * scale
        q_unit[:, lanes] = unit
        q_scale[:, lanes] = scale
        normed = (unit * gain_q).astype(BF).astype(F32) * 0.125
        if pair < 8:
            qg_stage[pair // 2, (pair % 2) * 2] = normed.astype(BF)
            qg_stage[pair // 2, (pair % 2) * 2 + 1] = g_in[0, :, lanes]
        else:
            upstream = g_in[0, :, lanes].astype(F32)
            for which in range(2):
                qg_stage[(pair - 8) * 2 + which, 4] = pick(normed, upstream, which)
    for d in range(1, NX):
        qg_x(d).start()
    qg[x] = qg_stage[x]

    def z_slot(offset):
        return (z + offset + NZ) % NZ

    def ag_up(s):
        ref = kv.at[:, z_slot(1 - s), core]
        return remote(ref, ref, sem_us.at[s - 1], sem_ur.at[s - 1], up)

    def ag_down(s):
        ref = kv.at[:, z_slot(s - 1), core]
        return remote(ref, ref, sem_ds.at[s - 1], sem_dr.at[s - 1], down)

    def ag_partner(i, offset):
        ref = kv.at[:, z_slot(offset), core]
        return remote(ref, ref, sem_ps.at[i], sem_pr.at[i], partner)

    for d in range(1, NX):
        kv_x(d).wait_recv()
    ag_up(1).start()
    ag_down(1).start()
    ag_partner(0, 0).start()

    def head_blocks(h):
        single = (h == 4).astype(jnp.int32)
        base = (h // 2) * 2
        q_block = base
        g_block = base + 1 - single
        q_lane = (h % 2) * 64
        g_lane = q_lane + 64 * single
        return q_block, g_block, pl.multiple_of(q_lane, 64), pl.multiple_of(g_lane, 64)

    def cell_rows(block, first, second):
        return jnp.concatenate(
            [kv[block, first].reshape(256, 128), kv[block, second].reshape(256, 128)], axis=0
        )

    def value_rows(block, g_lane, first, second):
        rows = cell_rows(block, first, second)
        mine = (lane < 64) == (g_lane < 64)
        return jnp.where(mine, rows, jnp.ones_like(rows))

    def forward(first, second):
        def body(h, carry):
            q_block, g_block, q_lane, g_lane = head_blocks(h)
            scores = dot_t(qm[h], cell_rows(q_block, first, second))
            weights = jnp.exp(scores).astype(BF)
            es[h, first] = weights[:, :256]
            es[h, second] = weights[:, 256:]
            acc[h] += dot(weights, value_rows(g_block, g_lane, first, second))
            return carry

        lax.fori_loop(0, 5, body, 0)

    def forward_pair(s):
        forward(z_slot(-s), z_slot(s - 1))

    def wait_partner(indices):
        for i in indices:
            ag_partner(i, 0).wait_recv()

    acc[...] = jnp.zeros_like(acc)
    gq_acc[...] = jnp.zeros_like(gq_acc)
    for s in range(1, 5):
        ag_up(s).wait_recv()
        if s < 4:
            ag_up(s + 1).start()
        ag_partner(2 * s - 1, -s).start()
        if s < 4:
            ag_down(s).wait_recv()
            if s < 3:
                ag_down(s + 1).start()
            ag_partner(2 * s, s).start()
        if s == 1:
            for d in range(1, NX):
                qg_x(d).wait_recv()
            for h, (q_block, g_block, q_lane, g_lane) in enumerate(HEADS):
                rows = qg[:, q_block].reshape(512, 128)
                qm[h] = jnp.where(low == (q_lane < 64), rows, jnp.zeros_like(rows))
        if s == 2:
            wait_partner((0, 1))
            forward_pair(1)
        if s == 3:
            wait_partner((2, 3))
            forward_pair(2)
            wait_partner((4, 5))
            forward_pair(3)
        if s == 4:
            wait_partner((6, 7))
            forward_pair(4)

    attended = []
    for h, (q_block, g_block, q_lane, g_lane) in enumerate(HEADS):
        mine = low == (g_lane < 64)
        total = acc[h]
        inverse = pltpu.roll(1.0 / total, 64, 1)
        weighted = jnp.where(mine, total * inverse, 0.0).astype(BF)
        scaled = jnp.where(mine, qg[:, g_block].reshape(512, 128).astype(F32) * inverse, 0.0).astype(BF)
        inner = jnp.sum(scaled.astype(F32) * weighted.astype(F32), axis=1, keepdims=True)
        high, rest = split(inner)
        spare = 64 - g_lane
        gm[h] = jnp.where(
            mine,
            scaled,
            jnp.where(lane == spare, -high, jnp.where(lane == spare + 1, -rest, jnp.zeros_like(scaled))),
        )
        q_t[h] = jnp.transpose(qm[h].astype(F32))[q_lane : q_lane + 64].astype(BF)
        g_t[h] = jnp.transpose(scaled.astype(F32))[g_lane : g_lane + 64].astype(BF)
        if h == 0 or h == 2:
            held = weighted
        elif h == 4:
            out_stage[:, 4] = weighted.reshape(4, 128, 128)
        else:
            out_stage[:, h // 2] = jnp.where(low, held, weighted).reshape(4, 128, 128)

    def out_x(part, d):
        blocks = pl.ds(0, 2) if part == 0 else pl.ds(2, 3)
        return remote(
            out_stage.at[(x + d) % NX, blocks],
            out_recv.at[x, blocks],
            sem_xs.at[2 + part, d - 1],
            sem_xr.at[2 + part, d - 1],
            x_peers[d - 1],
        )

    for d in range(1, NX):
        out_x(0, d).start()

    def backward(step, first, second, start, stop):
        def body(h, carry):
            q_block, g_block, q_lane, g_lane = head_blocks(h)
            keys = cell_rows(q_block, first, second)
            weights = jnp.concatenate([es[h, first], es[h, second]], axis=1)
            change = dot_t(gm[h], value_rows(g_block, g_lane, first, second))
            grads = (change * weights.astype(F32)).astype(BF)
            gq_acc[h] += dot(grads, keys)
            key_part = dot(q_t[h], grads)
            value_part = dot(g_t[h], weights)
            for i in range(2):
                for c in range(2):
                    cols = slice(i * 256 + c * 128, i * 256 + c * 128 + 128)
                    g_all[step, i, c, q_block, pl.ds(q_lane, 64), :] = key_part[:, cols]
                    g_all[step, i, c, g_block, pl.ds(g_lane, 64), :] = value_part[:, cols]
            return carry

        lax.fori_loop(start, stop, body, 0)

    def core_copy(step):
        return remote(core_send.at[step], core_recv.at[step], sem_cs.at[step], sem_cr.at[step], partner)

    def rs_up(step):
        return remote(up_send.at[step], up_recv.at[step], sem_rus.at[step], sem_rur.at[step], up)

    def rs_down(step):
        return remote(dn_send.at[step], dn_recv.at[step], sem_rds.at[step], sem_rdr.at[step], down)

    def reduce_step(step):
        core_copy(step).wait_recv()
        upward = g_all[step, 0, core] + core_recv[step, 0].astype(F32)
        if step > 0:
            rs_up(step - 1).wait_recv()
            upward = upward + up_recv[step - 1].astype(F32)
        up_send[step] = upward.astype(BF)
        rs_up(step).start()
        if step < 3:
            downward = g_all[step, 1, core] + core_recv[step, 1].astype(F32)
            if step > 0:
                rs_down(step - 1).wait_recv()
                downward = downward + dn_recv[step - 1].astype(F32)
            dn_send[step] = downward.astype(BF)
            rs_down(step).start()

    for step in range(4):
        first, second = z_slot(4 - step), z_slot(step - 3)
        if step == 0:
            backward(step, first, second, 0, 5)
        else:
            backward(step, first, second, 0, 3)
            reduce_step(step - 1)
            backward(step, first, second, 3, 5)
        core_send[step] = g_all[step, :, other].astype(BF)
        core_copy(step).start()

    for h in (0, 2):
        out_stage[:, 2 + h // 2] = (
            jnp.where(low, gq_acc[h], gq_acc[h + 1]).astype(BF).reshape(4, 128, 128)
        )
    out_stage[:, 4] = jnp.where(
        low, gq_acc[4], out_stage[:, 4].reshape(512, 128).astype(F32)
    ).astype(BF).reshape(4, 128, 128)
    for d in range(1, NX):
        out_x(1, d).start()
    out_recv[x] = out_stage[x]
    reduce_step(3)

    for part in range(2):
        for d in range(1, NX):
            out_x(part, d).wait_recv()

    def join(first, second, which):
        if which == 0:
            return jnp.where(low, first, pltpu.roll(second, 64, 1))
        return jnp.where(low, pltpu.roll(first, 64, 1), second)

    q_terms = jnp.zeros((8, 128), F32)
    for pair in range(10):
        lanes = slice(pair * 128, pair * 128 + 128)
        if pair < 8:
            att_out[0, :, lanes] = out_recv[pair // 2, pair % 2]
            grad = out_recv[pair // 2, 2 + pair % 2].astype(F32)
        else:
            one = out_recv[(pair - 8) * 2, 4].astype(F32)
            two = out_recv[(pair - 8) * 2 + 1, 4].astype(F32)
            att_out[0, :, lanes] = join(one, two, 1).astype(BF)
            grad = join(one, two, 0)
        grad = grad * 0.125
        unit = q_unit[:, lanes]
        product = grad * unit
        q_terms = q_terms + jnp.sum(product.reshape(16, 8, 128), axis=0)
        inner = head_mean(product * gain_q)
        gq_out[0, :, lanes] = (q_scale[:, lanes] * (grad * gain_q - unit * inner)).astype(BF)

    rs_up(3).wait_recv()
    rs_down(2).wait_recv()
    for b in range(5):
        final = (
            g_all[3, 1, core, b]
            + core_recv[3, 1, b].astype(F32)
            + up_recv[3, b].astype(F32)
            + dn_recv[2, b].astype(F32)
        )
        cell_stage[b] = jnp.transpose(final).astype(BF)

    def cell_x(d):
        rows = pl.ds(pl.multiple_of(((x + d) % NX) * 32, 32), 32)
        return remote(
            cell_stage.at[:, rows, :], cell_recv.at[x], sem_xs.at[4, d - 1], sem_xr.at[4, d - 1], x_peers[d - 1]
        )

    for d in range(1, NX):
        cell_x(d).start()
    cell_recv[x] = cell_stage[:, pl.ds(pl.multiple_of(x * 32, 32), 32), :]
    cell = seq * 32 + lax.broadcasted_iota(jnp.int32, (32, 1), 0)
    table = (unmerge_in[...] == cell).astype(F32).astype(BF)
    for d in range(1, NX):
        cell_x(d).wait_recv()

    k_terms = jnp.zeros((8, 128), F32)
    for pair in range(10):
        lanes = slice(pair * 128, pair * 128 + 128)
        if pair < 8:
            cell_k = cell_recv[pair // 2, (pair % 2) * 2]
            cell_v = cell_recv[pair // 2, (pair % 2) * 2 + 1]
        else:
            one = cell_recv[(pair - 8) * 2, 4].astype(F32)
            two = cell_recv[(pair - 8) * 2 + 1, 4].astype(F32)
            cell_k = join(one, two, 0).astype(BF)
            cell_v = join(one, two, 1).astype(BF)
        gv_out[0, :, lanes] = (dot_l(table, cell_v) * 0.25).astype(BF)
        grad = dot_l(table, cell_k) * 0.25
        unit = k_unit[:, lanes]
        product = grad * unit
        k_terms = k_terms + jnp.sum(product.reshape(16, 8, 128), axis=0)
        inner = head_mean(product * gain_k)
        gk_out[0, :, lanes] = (k_scale[:, lanes] * (grad * gain_k - unit * inner)).astype(BF)

    q_row = jnp.sum(q_terms, axis=0, keepdims=True)
    k_row = jnp.sum(k_terms, axis=0, keepdims=True)
    q_row = q_row + pltpu.roll(q_row, 64, 1)
    k_row = k_row + pltpu.roll(k_row, 64, 1)
    value = jnp.broadcast_to(jnp.where(low, q_row, k_row), (8, 128))

    def total_over(value, slot, stage, base, buffer, mine, peers, count):
        gain_own[stage] = value
        copies = []
        for i, device in enumerate(peers):
            copies.append(
                remote(
                    gain_own.at[stage], buffer.at[mine], sem_gs.at[base + i], sem_gr.at[base + i], device
                )
            )
        for copy in copies:
            copy.start()
        buffer[mine] = value
        for copy in copies:
            copy.wait_recv()
        result = buffer[0]
        for i in range(1, count):
            result = result + buffer[i]
        return result

    value = total_over(value, core, 0, 0, gain_core, core, [partner], 2)
    value = total_over(value, x, 1, 1, gain_x, x, x_peers, NX)
    if ny > 1:
        value = total_over(value, img, 2, 4, gain_y, img, y_peers, ny)
    value = total_over(value, z, 3, 7, gain_z, z, z_peers, NZ)
    gain_out[...] = value

    for d in range(1, NX):
        kv_x(d).wait_send()
        qg_x(d).wait_send()
        out_x(0, d).wait_send()
        out_x(1, d).wait_send()
        cell_x(d).wait_send()
    for s in range(1, 5):
        ag_up(s).wait_send()
        if s < 4:
            ag_down(s).wait_send()
    for i in range(8):
        ag_partner(i, 0).wait_send()
    for step in range(4):
        core_copy(step).wait_send()
        rs_up(step).wait_send()
        if step < 3:
            rs_down(step).wait_send()
    tile = gain_own.at[0]
    for i in range(1 + (NX - 1) + (ny - 1) + (NZ - 1)):
        slot = i if ny > 1 or i < 4 else i + 3
        remote(tile, tile, sem_gs.at[slot], sem_gr.at[slot], partner).wait_send()


def local(ny, query_proj, key_proj, value_proj, merge_cells, unmerge, grad_out, query_gain, key_gain):
    vmem = pltpu.VMEM
    dma = pltpu.SemaphoreType.DMA
    block = (5, 128, 128)
    outs = pl.pallas_call(
        functools.partial(kernel, ny),
        out_shape=[jax.ShapeDtypeStruct((1, 128, 1280), BF)] * 4
        + [jax.ShapeDtypeStruct((8, 128), F32)],
        in_specs=[pl.BlockSpec(memory_space=pltpu.VMEM)] * 8,
        out_specs=[pl.BlockSpec(memory_space=pltpu.VMEM)] * 5,
        scratch_shapes=[
            vmem((128, 1280), F32),
            vmem((128, 1280), F32),
            vmem((128, 1280), F32),
            vmem((128, 1280), F32),
            vmem((4, 5, 32, 128), BF),
            vmem((4,) + block, BF),
            vmem((5, 8, 2, 128, 128), BF),
            vmem((4,) + block, BF),
            vmem((5, 512, 128), BF),
            vmem((5, 512, 128), BF),
            vmem((5, 64, 512), BF),
            vmem((5, 64, 512), BF),
            vmem((5, 8, 512, 256), BF),
            vmem((5, 512, 128), F32),
            vmem((5, 512, 128), F32),
            vmem((4, 2, 2) + block, F32),
            vmem((4, 2) + block, BF),
            vmem((4, 2) + block, BF),
            vmem((4,) + block, BF),
            vmem((4,) + block, BF),
            vmem((3,) + block, BF),
            vmem((3,) + block, BF),
            vmem((4,) + block, BF),
            vmem((4,) + block, BF),
            vmem(block, BF),
            vmem((4, 5, 32, 128), BF),
            vmem((4, 8, 128), F32),
            vmem((2, 8, 128), F32),
            vmem((NX, 8, 128), F32),
            vmem((max(ny, 2), 8, 128), F32),
            vmem((NZ, 8, 128), F32),
            dma((5, 3)),
            dma((5, 3)),
            dma((4,)),
            dma((4,)),
            dma((3,)),
            dma((3,)),
            dma((8,)),
            dma((8,)),
            dma((4,)),
            dma((4,)),
            dma((4,)),
            dma((4,)),
            dma((3,)),
            dma((3,)),
            dma((14,)),
            dma((14,)),
        ],
        compiler_params=pltpu.CompilerParams(
            collective_id=0, has_side_effects=True, vmem_limit_bytes=60 * 1024 * 1024
        ),
        name="attention_block",
    )(
        query_proj,
        key_proj,
        value_proj,
        merge_cells,
        unmerge,
        grad_out,
        query_gain.reshape(1, 64),
        key_gain.reshape(1, 64),
    )
    return (outs[0], outs[1], outs[2], outs[3], outs[4][0, :64], outs[4][0, 64:])


def solution(mesh):
    placed = (
        P("img", "seq", None),
        P("img", "seq", None),
        P("img", "seq", None),
        P("img", "seq", None),
        P("img", "seq"),
        P("img", "seq", None),
        P(),
        P(),
    )
    return jax.shard_map(
        functools.partial(local, mesh.shape["img"]),
        mesh=mesh,
        in_specs=placed,
        out_specs=(
            P("img", "seq", None),
            P("img", "seq", None),
            P("img", "seq", None),
            P("img", "seq", None),
            P(),
            P(),
        ),
        check_vma=False,
    )
```

time: 1620 us -> 94.8 us (0.06)
  waiting for transfers between devices: 1280 us -> 0 us
  local copies, waits for them, and re-layouts: 124 us -> 7.38 us
  matrix products: 93.7 us -> 0 us
  Pallas kernels: 0 us -> 86.6 us
  blocking collectives: 79.5 us -> 0 us
  other arithmetic: 16.3 us -> 0 us
    all_gather x10 -> x0, waiting for transfers between devices: 666 us -> none  [the longest x5 362 us: local(): lax.all_gather(v_merged[:, lane_start:lane_start + group_lanes], 'seq', a...]
    reduce_scatter x5 -> x0, waiting for transfers between devices: 609 us -> none  [local(): lax.psum_scatter(term_rows, 'seq', scatter_dimension=0, tiled=True)]
    dot_general x144 -> x0, matrix products: 93.7 us -> none  [the longest x40 35.5 us: scores_of(): jnp.einsum('thd,khd->thk', queries, key_rows.reshape(-1, group_heads, hea...]
    pallas_call x0 -> x1, Pallas kernels: none -> 86.6 us  [local(): pl.pallas_call(functools.partial(kernel, ny), out_shape=[jax.ShapeDtypeSt...]
    psum x1 -> x0, blocking collectives: 79.5 us -> none  [local(): lax.psum((gain_terms[0], gain_terms[1]), ('img', 'seq'))]
    dynamic_slice x40 -> x0, local copies, waits for them, and re-layouts: 42.7 us -> none  [attention_pass(): lax.scan(forward_step, initial, (key_blocks, value_blocks))]
    dynamic_update_slice x40 -> x0, local copies, waits for them, and re-layouts: 27.8 us -> none  [attention_pass(): lax.scan(backward_step, query_zero, (key_blocks, value_blocks))]
    unnamed x111 -> x11, local copies, waits for them, and re-layouts: 32.6 us -> 6.04 us
  transfers between devices with their start and end apart: 15 -> 0, of which waited for: 15 -> 0; matrix products, arithmetic and copies ran while one was open for 14% -> 0% of each run, Pallas kernels for 0% -> 0%
where the time goes in v1:
time: 94.8 us; the launch traced here: 94.6 us
  Pallas kernels  86.6 us (91%)
  local copies, waits for them, and re-layouts  7.38 us (8%)
    pallas_call x1, Pallas kernels, local(): pl.pallas_call(functools.partial(kernel, ny), out_shape=[jax.ShapeDtypeSt...  86.6 us
    unnamed x11, local copies, waits for them, and re-layouts  6.04 us

profile of v1, /device:TPU:1, one launch (start us, length us, event | category | flops | bytes accessed | tf_op | source)
XLA Modules:
  0.0 94.6 jit_solution(17151276793533834978)
XLA Ops:
  0.6 1.4 %copy.14.merge_in = s32[1,32,4]{2,1,0:T(8,128)} copy(s32[1,32,4]{1,2,0:T(4,128)} %param.11) | data formatting | bytes 1024 | tf_op args[3]
  2.0 86.6 %attention_block.1 = (bf16[1,128,1280]{2,1,0:T(8,128)(2,1)}, bf16[1,128,1280]{2,1,0:T(8,128)(2,1)}, bf16[1,128,1280]{2,1,0:T(8,128)(2,1)}, bf16[1,128,1280]{2,1,0:T(8,128)(2,1)}, f32[8,128]{1,0:T(8,128)}) custom-call(bf16[1,128,1280]{2,1,0:T(8,128)(2,1)} %q_in.1, bf16[1,128,1280]{2,1,0:T(8,128)(2,1)} %k_in.1, bf16[1,128,1280]{2,1,0:T(8,128)(2,1)} %v_in.1, ...), custom_call_target="tpu_custom_call" | custom-call | tf_op jit(solution)/shard_map/attention_block/pallas_call | solution.py:530
  88.6 1.3 %slice_bitcast_fusion = (f32[64]{0:T(128)}, f32[64]{0:T(128)}) fusion(f32[8,128]{1,0:T(8,128)} %get-tuple-element.15), kind=kLoop, calls=%fused_computation | loop fusion | bytes 1024 | tf_op jit(solution)/shard_map/squeeze | solution.py:599
  89.9 0.0 copy-start.2
  89.9 1.8 %copy.19 = bf16[1,128,1280]{2,1,0:T(8,128)(2,1)} copy(bf16[1,128,1280]{2,1,0:T(8,128)(2,1)} %get-tuple-element.24) | data formatting | bytes 655360
  91.7 0.0 copy-done.2
  91.7 0.0 copy-start.1
  91.7 0.7 copy.20
  92.4 0.4 copy-done.1
  92.8 0.0 copy-start
  92.8 0.7 copy.21
  93.5 0.4 copy-done
  93.9 0.7 copy.22
Async XLA Ops:
  89.9 1.8 %copy-start.2 = (bf16[1,128,1280]{2,1,0:T(8,128)(2,1)S(1)}, bf16[1,128,1280]{2,1,0:T(8,128)(2,1)}, u32[]{:S(2)}) copy-start(bf16[1,128,1280]{2,1,0:T(8,128)(2,1)} %get-tuple-element.25) | copy-start | bytes 983044
  91.7 1.1 %copy-start.1 = (bf16[1,128,1280]{2,1,0:T(8,128)(2,1)S(1)}, bf16[1,128,1280]{2,1,0:T(8,128)(2,1)}, u32[]{:S(2)}) copy-start(bf16[1,128,1280]{2,1,0:T(8,128)(2,1)} %get-tuple-element.26) | copy-start | bytes 983044
  92.8 1.1 %copy-start = (bf16[1,128,1280]{2,1,0:T(8,128)(2,1)S(1)}, bf16[1,128,1280]{2,1,0:T(8,128)(2,1)}, u32[]{:S(2)}) copy-start(bf16[1,128,1280]{2,1,0:T(8,128)(2,1)} %get-tuple-element.27) | copy-start | bytes 983044

commit v2 on v1

v2 whole, which is shorter than its diff:
```python
import functools

import jax
import jax.numpy as jnp
from jax import lax
from jax.experimental import pallas as pl
from jax.experimental.pallas import tpu as pltpu
from jax.sharding import PartitionSpec as P

BF = jnp.bfloat16
F32 = jnp.float32
EPSILON = 1e-06
NZ, NX = 8, 4
HEADS = ((0, 1, 0, 0), (0, 1, 64, 64), (2, 3, 0, 0), (2, 3, 64, 64), (4, 4, 0, 64))
Q_AT = {0: 0, 2: 1, 4: 2, 1: 3, 3: 4}
PARTS = ((0, 2), (2, 3))


def dot(a, b):
    return jnp.dot(a, b, preferred_element_type=F32)


def dot_t(a, b):
    return lax.dot_general(a, b, (((1,), (1,)), ((), ())), preferred_element_type=F32)


def dot_l(a, b):
    return lax.dot_general(a, b, (((0,), (0,)), ((), ())), preferred_element_type=F32)


def split(value):
    high = value.astype(BF)
    return high, (value - high.astype(F32)).astype(BF)


def kernel(
    ny,
    q_in,
    k_in,
    v_in,
    unmerge_in,
    g_in,
    q_gain,
    k_gain,
    att_out,
    gq_out,
    gk_out,
    gv_out,
    gain_out,
    q_unit,
    q_scale,
    k_unit,
    k_scale,
    kv_stage,
    qg_stage,
    kv,
    qg,
    qm,
    gm,
    q_t,
    g_t,
    es,
    acc,
    gq_acc,
    g_all,
    core_send,
    core_recv,
    up_send,
    up_recv,
    dn_send,
    dn_recv,
    out_stage,
    out_recv,
    cell_stage,
    cell_recv,
    gain_own,
    gain_core,
    gain_x,
    gain_y,
    gain_z,
    sem_xs,
    sem_xr,
    sem_us,
    sem_ur,
    sem_ds,
    sem_dr,
    sem_ps,
    sem_pr,
    sem_cs,
    sem_cr,
    sem_rus,
    sem_rur,
    sem_rds,
    sem_rdr,
    sem_gs,
    sem_gr,
):
    img = lax.axis_index("img")
    seq = lax.axis_index("seq")
    core = seq % 2
    x = (seq // 2) % NX
    z = seq // (2 * NX)
    other = 1 - core

    def at(zz, xx, cc):
        return (img, (zz * NX + xx) * 2 + cc)

    up = at((z + 1) % NZ, x, core)
    down = at((z + NZ - 1) % NZ, x, core)
    partner = at(z, x, other)
    x_peers = [at(z, (x + d) % NX, core) for d in range(1, NX)]
    z_peers = [at((z + d) % NZ, x, core) for d in range(1, NZ)]
    y_peers = [((img + d) % ny, seq) for d in range(1, ny)]
    barrier = pltpu.get_barrier_semaphore()
    greeted = [partner] + x_peers + z_peers + y_peers
    for device in greeted:
        pl.semaphore_signal(barrier, inc=1, device_id=device, device_id_type=pl.DeviceIdType.MESH)

    def remote(src, dst, send_sem, recv_sem, device):
        return pltpu.make_async_remote_copy(
            src_ref=src,
            dst_ref=dst,
            send_sem=send_sem,
            recv_sem=recv_sem,
            device_id=device,
            device_id_type=pl.DeviceIdType.MESH,
        )

    lane = lax.broadcasted_iota(jnp.int32, (1, 128), 1)
    low = lane < 64
    head_sum = (
        (lax.broadcasted_iota(jnp.int32, (128, 128), 0) < 64)
        == (lax.broadcasted_iota(jnp.int32, (128, 128), 1) < 64)
    ).astype(F32).astype(BF)

    def head_mean(value):
        high, rest = split(value)
        return (dot(high, head_sum) + dot(rest, head_sum)) * (1.0 / 64.0)

    gain_q = jnp.concatenate([q_gain[...], q_gain[...]], axis=1)
    gain_k = jnp.concatenate([k_gain[...], k_gain[...]], axis=1)
    cell = seq * 32 + lax.broadcasted_iota(jnp.int32, (32, 1), 0)
    member = (unmerge_in[...] == cell).astype(F32).astype(BF)

    def pick(first, second, which):
        if which == 0:
            return jnp.where(low, first, pltpu.roll(second, 64, 1)).astype(BF)
        return jnp.where(low, pltpu.roll(first, 64, 1), second).astype(BF)

    for pair in range(10):
        lanes = slice(pair * 128, pair * 128 + 128)
        raw = k_in[0, :, lanes].astype(F32)
        scale = lax.rsqrt(head_mean(raw * raw) + EPSILON)
        unit = raw * scale
        k_unit[:, lanes] = unit
        k_scale[:, lanes] = scale
        high, rest = split(unit * gain_k)
        merged_k = (dot(member, high) + dot(member, rest)) * 0.25
        merged_v = dot(member, v_in[0, :, lanes]) * 0.25
        if pair < 8:
            kv_stage[pair // 2, (pair % 2) * 2] = merged_k.astype(BF)
            kv_stage[pair // 2, (pair % 2) * 2 + 1] = merged_v.astype(BF)
        else:
            for which in range(2):
                kv_stage[(pair - 8) * 2 + which, 4] = pick(merged_k, merged_v, which)
    pl.semaphore_wait(barrier, len(greeted))

    def kv_x(d):
        return remote(
            kv_stage.at[(x + d) % NX],
            kv.at[:, z, core, pl.ds(pl.multiple_of(x * 32, 32), 32), :],
            sem_xs.at[0, d - 1],
            sem_xr.at[0, d - 1],
            x_peers[d - 1],
        )

    def qg_x(part, d):
        blocks = pl.ds(0, 3) if part == 0 else pl.ds(3, 2)
        return remote(
            qg_stage.at[(x + d) % NX, blocks],
            qg.at[x, blocks],
            sem_xs.at[1 + part, d - 1],
            sem_xr.at[1 + part, d - 1],
            x_peers[d - 1],
        )

    for d in range(1, NX):
        kv_x(d).start()
    kv[:, z, core, pl.ds(pl.multiple_of(x * 32, 32), 32), :] = kv_stage[x]
    for pair in range(10):
        lanes = slice(pair * 128, pair * 128 + 128)
        raw = q_in[0, :, lanes].astype(F32)
        scale = lax.rsqrt(head_mean(raw * raw) + EPSILON)
        unit = raw * scale
        q_unit[:, lanes] = unit
        q_scale[:, lanes] = scale
        normed = (unit * gain_q).astype(BF).astype(F32) * 0.125
        if pair < 8:
            qg_stage[pair // 2, pair % 2] = normed.astype(BF)
        else:
            upstream = g_in[0, :, lanes].astype(F32)
            for which in range(2):
                qg_stage[(pair - 8) * 2 + which, 2] = pick(normed, upstream, which)
    for d in range(1, NX):
        qg_x(0, d).start()
    for pair in range(8):
        qg_stage[pair // 2, 3 + pair % 2] = g_in[0, :, pair * 128 : pair * 128 + 128]
    for d in range(1, NX):
        qg_x(1, d).start()
    qg[x] = qg_stage[x]

    def z_slot(offset):
        return (z + offset + NZ) % NZ

    def blocks_of(part):
        return pl.ds(*PARTS[part])

    def ag_up(s, part):
        ref = kv.at[blocks_of(part), z_slot(1 - s), core]
        return remote(ref, ref, sem_us.at[s - 1, part], sem_ur.at[s - 1, part], up)

    def ag_down(s, part):
        ref = kv.at[blocks_of(part), z_slot(s - 1), core]
        return remote(ref, ref, sem_ds.at[s - 1, part], sem_dr.at[s - 1, part], down)

    def ag_partner(i, offset, part):
        ref = kv.at[blocks_of(part), z_slot(offset), core]
        return remote(ref, ref, sem_ps.at[i, part], sem_pr.at[i, part], partner)

    def on_up(s, part):
        return s < 4 or part == 0

    def on_down(s, part):
        return s < 4 or part == 1

    def gather_hop(s, part):
        if on_up(s, part):
            ag_up(s, part).wait_recv()
            if s < 4 and on_up(s + 1, part):
                ag_up(s + 1, part).start()
            ag_partner(2 * s - 1, -s, part).start()
        if on_down(s, part):
            ag_down(s, part).wait_recv()
            if s < 4 and on_down(s + 1, part):
                ag_down(s + 1, part).start()
            ag_partner(2 * s if s < 4 else 7, s, part).start()

    for d in range(1, NX):
        kv_x(d).wait_recv()
    for part in range(2):
        ag_up(1, part).start()
        ag_down(1, part).start()
    for part in range(2):
        ag_partner(0, 0, part).start()

    def head_blocks(h):
        single = (h == 4).astype(jnp.int32)
        base = (h // 2) * 2
        q_block = base
        g_block = base + 1 - single
        q_lane = (h % 2) * 64
        g_lane = q_lane + 64 * single
        return q_block, g_block, pl.multiple_of(q_lane, 64), pl.multiple_of(g_lane, 64)

    def cell_rows(block, first, second):
        return jnp.concatenate(
            [kv[block, first].reshape(256, 128), kv[block, second].reshape(256, 128)], axis=0
        )

    def value_rows(block, g_lane, first, second):
        rows = cell_rows(block, first, second)
        mine = (lane < 64) == (g_lane < 64)
        return jnp.where(mine, rows, jnp.ones_like(rows))

    def forward(first, second, start, stop):
        def body(h, carry):
            q_block, g_block, q_lane, g_lane = head_blocks(h)
            scores = dot_t(qm[h], cell_rows(q_block, first, second))
            weights = jnp.exp(scores).astype(BF)
            es[h, first] = weights[:, :256]
            es[h, second] = weights[:, 256:]
            acc[h] += dot(weights, value_rows(g_block, g_lane, first, second))
            return carry

        lax.fori_loop(start, stop, body, 0)

    def forward_pair(s, start, stop):
        forward(z_slot(-s), z_slot(s - 1), start, stop)

    def wait_partner(indices):
        for i in indices:
            for part in range(2):
                ag_partner(i, 0, part).wait_recv()

    acc[...] = jnp.zeros_like(acc)
    gq_acc[...] = jnp.zeros_like(gq_acc)
    gather_hop(1, 0)
    gather_hop(1, 1)
    for d in range(1, NX):
        qg_x(0, d).wait_recv()
    for h, (q_block, g_block, q_lane, g_lane) in enumerate(HEADS):
        rows = qg[:, Q_AT[q_block]].reshape(512, 128)
        qm[h] = jnp.where(low == (q_lane < 64), rows, jnp.zeros_like(rows))
        if h == 1:
            gather_hop(2, 0)
    wait_partner((0, 1))
    forward_pair(1, 0, 2)
    gather_hop(2, 1)
    forward_pair(1, 2, 5)
    gather_hop(3, 0)
    wait_partner((2, 3))
    forward_pair(2, 0, 2)
    gather_hop(3, 1)
    forward_pair(2, 2, 5)
    gather_hop(4, 0)
    gather_hop(4, 1)
    for h, (q_block, g_block, q_lane, g_lane) in enumerate(HEADS):
        q_t[h] = jnp.transpose(qm[h].astype(F32))[q_lane : q_lane + 64].astype(BF)
    wait_partner((4, 5))
    forward_pair(3, 0, 5)
    wait_partner((6, 7))
    forward_pair(4, 0, 5)
    for d in range(1, NX):
        qg_x(1, d).wait_recv()

    attended = []
    for h, (q_block, g_block, q_lane, g_lane) in enumerate(HEADS):
        mine = low == (g_lane < 64)
        total = acc[h]
        inverse = pltpu.roll(1.0 / total, 64, 1)
        weighted = jnp.where(mine, total * inverse, 0.0).astype(BF)
        scaled = jnp.where(mine, qg[:, Q_AT[g_block]].reshape(512, 128).astype(F32) * inverse, 0.0).astype(BF)
        inner = jnp.sum(scaled.astype(F32) * weighted.astype(F32), axis=1, keepdims=True)
        high, rest = split(inner)
        spare = 64 - g_lane
        gm[h] = jnp.where(
            mine,
            scaled,
            jnp.where(lane == spare, -high, jnp.where(lane == spare + 1, -rest, jnp.zeros_like(scaled))),
        )
        g_t[h] = jnp.transpose(scaled.astype(F32))[g_lane : g_lane + 64].astype(BF)
        if h == 0 or h == 2:
            held = weighted
        elif h == 4:
            out_stage[:, 4] = weighted.reshape(4, 128, 128)
        else:
            out_stage[:, h // 2] = jnp.where(low, held, weighted).reshape(4, 128, 128)

    def out_x(part, d):
        blocks = pl.ds(*((0, 2), (2, 1), (3, 2))[part])
        return remote(
            out_stage.at[(x + d) % NX, blocks],
            out_recv.at[x, blocks],
            sem_xs.at[3 + part, d - 1],
            sem_xr.at[3 + part, d - 1],
            x_peers[d - 1],
        )

    for d in range(1, NX):
        out_x(0, d).start()

    def backward(step, first, second, start, stop):
        def body(h, carry):
            q_block, g_block, q_lane, g_lane = head_blocks(h)
            keys = cell_rows(q_block, first, second)
            weights = jnp.concatenate([es[h, first], es[h, second]], axis=1)
            change = dot_t(gm[h], value_rows(g_block, g_lane, first, second))
            grads = (change * weights.astype(F32)).astype(BF)
            gq_acc[h] += dot(grads, keys)
            key_part = dot(q_t[h], grads)
            value_part = dot(g_t[h], weights)
            for i in range(2):
                for c in range(2):
                    cols = slice(i * 256 + c * 128, i * 256 + c * 128 + 128)
                    g_all[step, i, c, q_block, pl.ds(q_lane, 64), :] = key_part[:, cols]
                    g_all[step, i, c, g_block, pl.ds(g_lane, 64), :] = value_part[:, cols]
            return carry

        lax.fori_loop(start, stop, body, 0)

    def core_copy(step, part):
        blocks = blocks_of(part)
        return remote(
            core_send.at[step, :, blocks],
            core_recv.at[step, :, blocks],
            sem_cs.at[step, part],
            sem_cr.at[step, part],
            partner,
        )

    def rs_up(hop, part):
        blocks = blocks_of(part)
        return remote(
            up_send.at[hop, blocks], up_recv.at[hop, blocks], sem_rus.at[hop, part], sem_rur.at[hop, part], up
        )

    def rs_down(hop, part):
        blocks = blocks_of(part)
        return remote(
            dn_send.at[hop, blocks], dn_recv.at[hop, blocks], sem_rds.at[hop, part], sem_rdr.at[hop, part], down
        )

    def chip_sum(step, i, part):
        blocks = blocks_of(part)
        return g_all[step, i, core, blocks] + core_recv[step, i, blocks].astype(F32)

    def send_up(hop, step, i, part):
        value = chip_sum(step, i, part)
        blocks = blocks_of(part)
        if hop > 0 and not (hop == 1 and part == 1):
            rs_up(hop - 1, part).wait_recv()
            value = value + up_recv[hop - 1, blocks].astype(F32)
        up_send[hop, blocks] = value.astype(BF)
        rs_up(hop, part).start()

    def send_down(hop, step, i, part):
        value = chip_sum(step, i, part)
        blocks = blocks_of(part)
        if hop > 0 and not (hop == 1 and part == 0):
            rs_down(hop - 1, part).wait_recv()
            value = value + dn_recv[hop - 1, blocks].astype(F32)
        dn_send[hop, blocks] = value.astype(BF)
        rs_down(hop, part).start()

    def reduce_half(step, part):
        core_copy(step, part).wait_recv()
        if step == 0 and part == 0:
            send_up(0, 0, 0, 0)
        elif step == 0:
            send_down(0, 0, 0, 1)
            send_up(1, 0, 1, 1)
        elif step == 1 and part == 0:
            send_down(1, 1, 0, 0)
            send_up(1, 0, 1, 0)
        elif step < 3:
            if step == 2 and part == 0:
                send_up(2, 1, 1, 0)
            send_down(step, step, 0, part)
            if part == 1:
                send_up(step + 1, step, 1, 1)
        else:
            if part == 0:
                send_up(3, 2, 1, 0)
            send_down(3, 3, 0, part)

    def backward_half(step, part):
        first = z_slot((4, -3, -2, -1)[step])
        second = z_slot((3, 2, 1, 0)[step])
        backward(step, first, second, *((0, 2), (2, 5))[part])
        blocks = blocks_of(part)
        core_send[step, :, blocks] = g_all[step, :, other, blocks].astype(BF)
        core_copy(step, part).start()

    for step in range(4):
        backward_half(step, 0)
        if step > 0:
            reduce_half(step - 1, 1)
        if step == 3:
            out_stage[:, 2] = jnp.where(low, gq_acc[0], gq_acc[1]).astype(BF).reshape(4, 128, 128)
            for d in range(1, NX):
                out_x(1, d).start()
        backward_half(step, 1)
        reduce_half(step, 0)

    out_stage[:, 3] = jnp.where(low, gq_acc[2], gq_acc[3]).astype(BF).reshape(4, 128, 128)
    out_stage[:, 4] = (
        jnp.where(low, gq_acc[4], out_stage[:, 4].reshape(512, 128).astype(F32))
        .astype(BF)
        .reshape(4, 128, 128)
    )
    for d in range(1, NX):
        out_x(2, d).start()
    out_recv[x] = out_stage[x]
    reduce_half(3, 1)

    def gain_copies(stage):
        base, buffer, mine, peers = gain_stages[stage]
        return [
            remote(gain_own.at[stage], buffer.at[mine], sem_gs.at[base + i], sem_gr.at[base + i], device)
            for i, device in enumerate(peers)
        ]

    def gain_send(stage, value):
        base, buffer, mine, peers = gain_stages[stage]
        gain_own[stage] = value
        for copy in gain_copies(stage):
            copy.start()
        buffer[mine] = value

    def gain_sum(stage):
        base, buffer, mine, peers = gain_stages[stage]
        for copy in gain_copies(stage):
            copy.wait_recv()
        result = buffer[0]
        for i in range(1, len(peers) + 1):
            result = result + buffer[i]
        return result

    gain_stages = (
        (0, gain_core, core, [partner]),
        (1, gain_x, x, x_peers),
        (4, gain_y, img, y_peers),
        (7, gain_z, z, z_peers),
    )
    tile = jnp.zeros((8, 128), F32)
    for h in range(5):
        tile = tile + jnp.sum((qm[h].astype(F32) * gq_acc[h]).reshape(64, 8, 128), axis=0)
    gain_send(0, tile)

    def join(first, second, which):
        if which == 0:
            return jnp.where(low, first, pltpu.roll(second, 64, 1))
        return jnp.where(low, pltpu.roll(first, 64, 1), second)

    def final_sum():
        for part in range(2):
            rs_up(3, part).wait_recv()
            rs_down(3, part).wait_recv()
        for b in range(5):
            total = (
                g_all[3, 1, core, b]
                + core_recv[3, 1, b].astype(F32)
                + up_recv[3, b].astype(F32)
                + dn_recv[3, b].astype(F32)
            )
            cell_stage[b] = jnp.transpose(total).astype(BF)

    def cell_x(d):
        rows = pl.ds(pl.multiple_of(((x + d) % NX) * 32, 32), 32)
        return remote(
            cell_stage.at[:, rows, :], cell_recv.at[x], sem_xs.at[6, d - 1], sem_xr.at[6, d - 1], x_peers[d - 1]
        )

    for d in range(1, NX):
        out_x(0, d).wait_recv()
    for pair in range(8):
        att_out[0, :, pair * 128 : pair * 128 + 128] = out_recv[pair // 2, pair % 2]
    gain_send(1, gain_sum(0))
    final_sum()
    for d in range(1, NX):
        cell_x(d).start()
    cell_recv[x] = cell_stage[:, pl.ds(pl.multiple_of(x * 32, 32), 32), :]
    gain_send(2, gain_sum(1))

    for part in (1, 2):
        for d in range(1, NX):
            out_x(part, d).wait_recv()
    for pair in range(10):
        lanes = slice(pair * 128, pair * 128 + 128)
        if pair < 8:
            grad = out_recv[pair // 2, 2 + pair % 2].astype(F32)
        else:
            one = out_recv[(pair - 8) * 2, 4].astype(F32)
            two = out_recv[(pair - 8) * 2 + 1, 4].astype(F32)
            att_out[0, :, lanes] = join(one, two, 1).astype(BF)
            grad = join(one, two, 0)
        grad = grad * 0.125 * gain_q
        unit = q_unit[:, lanes]
        inner = head_mean(grad * unit)
        gq_out[0, :, lanes] = (q_scale[:, lanes] * (grad - unit * inner)).astype(BF)
        if pair == 4:
            gain_send(3, gain_sum(2))

    for d in range(1, NX):
        cell_x(d).wait_recv()
    for pair in range(10):
        lanes = slice(pair * 128, pair * 128 + 128)
        if pair < 8:
            cell_k = cell_recv[pair // 2, (pair % 2) * 2]
            cell_v = cell_recv[pair // 2, (pair % 2) * 2 + 1]
        else:
            one = cell_recv[(pair - 8) * 2, 4].astype(F32)
            two = cell_recv[(pair - 8) * 2 + 1, 4].astype(F32)
            cell_k = join(one, two, 0).astype(BF)
            cell_v = join(one, two, 1).astype(BF)
        gv_out[0, :, lanes] = (dot_l(member, cell_v) * 0.25).astype(BF)
        grad = dot_l(member, cell_k) * 0.25 * gain_k
        unit = k_unit[:, lanes]
        inner = head_mean(grad * unit)
        gk_out[0, :, lanes] = (k_scale[:, lanes] * (grad - unit * inner)).astype(BF)

    row = jnp.sum(gain_sum(3), axis=0, keepdims=True)
    row = row + pltpu.roll(row, 64, 1)
    gain_out[...] = jnp.broadcast_to(row / jnp.where(low, gain_q, gain_k), (8, 128))

    for d in range(1, NX):
        kv_x(d).wait_send()
        for part in range(2):
            qg_x(part, d).wait_send()
        for part in range(3):
            out_x(part, d).wait_send()
        cell_x(d).wait_send()
    for part in range(2):
        for s in range(1, 5):
            if on_up(s, part):
                ag_up(s, part).wait_send()
                rs_up(4 - s, part).wait_send()
            if on_down(s, part):
                ag_down(s, part).wait_send()
                rs_down(4 - s, part).wait_send()
        for i in range(8):
            ag_partner(i, 0, part).wait_send()
        for step in range(4):
            core_copy(step, part).wait_send()
    for stage in range(4):
        for copy in gain_copies(stage):
            copy.wait_send()


def local(ny, query_proj, key_proj, value_proj, merge_cells, unmerge, grad_out, query_gain, key_gain):
    vmem = pltpu.VMEM
    dma = pltpu.SemaphoreType.DMA
    block = (5, 128, 128)
    outs = pl.pallas_call(
        functools.partial(kernel, ny),
        out_shape=[jax.ShapeDtypeStruct((1, 128, 1280), BF)] * 4
        + [jax.ShapeDtypeStruct((8, 128), F32)],
        in_specs=[pl.BlockSpec(memory_space=pltpu.VMEM)] * 7,
        out_specs=[pl.BlockSpec(memory_space=pltpu.VMEM)] * 5,
        scratch_shapes=[
            vmem((128, 1280), F32),
            vmem((128, 1280), F32),
            vmem((128, 1280), F32),
            vmem((128, 1280), F32),
            vmem((4, 5, 32, 128), BF),
            vmem((4,) + block, BF),
            vmem((5, 8, 2, 128, 128), BF),
            vmem((4,) + block, BF),
            vmem((5, 512, 128), BF),
            vmem((5, 512, 128), BF),
            vmem((5, 64, 512), BF),
            vmem((5, 64, 512), BF),
            vmem((5, 8, 512, 256), BF),
            vmem((5, 512, 128), F32),
            vmem((5, 512, 128), F32),
            vmem((4, 2, 2) + block, F32),
            vmem((4, 2) + block, BF),
            vmem((4, 2) + block, BF),
            vmem((4,) + block, BF),
            vmem((4,) + block, BF),
            vmem((4,) + block, BF),
            vmem((4,) + block, BF),
            vmem((4,) + block, BF),
            vmem((4,) + block, BF),
            vmem(block, BF),
            vmem((4, 5, 32, 128), BF),
            vmem((4, 8, 128), F32),
            vmem((2, 8, 128), F32),
            vmem((NX, 8, 128), F32),
            vmem((ny, 8, 128), F32),
            vmem((NZ, 8, 128), F32),
            dma((7, 3)),
            dma((7, 3)),
            dma((4, 2)),
            dma((4, 2)),
            dma((4, 2)),
            dma((4, 2)),
            dma((8, 2)),
            dma((8, 2)),
            dma((4, 2)),
            dma((4, 2)),
            dma((4, 2)),
            dma((4, 2)),
            dma((4, 2)),
            dma((4, 2)),
            dma((14,)),
            dma((14,)),
        ],
        compiler_params=pltpu.CompilerParams(
            collective_id=0, has_side_effects=True, vmem_limit_bytes=60 * 1024 * 1024
        ),
        name="attention_block",
    )(
        query_proj,
        key_proj,
        value_proj,
        unmerge,
        grad_out,
        query_gain.reshape(1, 64),
        key_gain.reshape(1, 64),
    )
    return (outs[0], outs[1], outs[2], outs[3], outs[4][0, :64], outs[4][0, 64:])


def solution(mesh):
    placed = (
        P("img", "seq", None),
        P("img", "seq", None),
        P("img", "seq", None),
        P("img", "seq", None),
        P("img", "seq"),
        P("img", "seq", None),
        P(),
        P(),
    )
    return jax.shard_map(
        functools.partial(local, mesh.shape["img"]),
        mesh=mesh,
        in_specs=placed,
        out_specs=(
            P("img", "seq", None),
            P("img", "seq", None),
            P("img", "seq", None),
            P("img", "seq", None),
            P(),
            P(),
        ),
        check_vma=False,
    )
```

time: 94.8 us -> 79.9 us (0.84)
  Pallas kernels: 86.6 us -> 73 us
  local copies, waits for them, and re-layouts: 7.38 us -> 6.01 us
    pallas_call x1, Pallas kernels: 86.6 us -> 73 us  [local(): pl.pallas_call(functools.partial(kernel, ny), out_shape=[jax.ShapeDtypeSt...]
    unnamed x11 -> x10, local copies, waits for them, and re-layouts: 6.04 us -> 4.67 us
where the time goes in v2:
time: 79.9 us; the launch traced here: 79.7 us
  Pallas kernels  73 us (91%)
  local copies, waits for them, and re-layouts  6.01 us (8%)
    pallas_call x1, Pallas kernels, local(): pl.pallas_call(functools.partial(kernel, ny), out_shape=[jax.ShapeDtypeSt...  73 us
    unnamed x10, local copies, waits for them, and re-layouts  4.67 us

profile of v2, /device:TPU:1, one launch (start us, length us, event | category | flops | bytes accessed | tf_op | source)
XLA Modules:
  0.0 79.7 jit_solution(3539412936053068517)
XLA Ops:
  0.6 73.0 %attention_block.1 = (bf16[1,128,1280]{2,1,0:T(8,128)(2,1)}, bf16[1,128,1280]{2,1,0:T(8,128)(2,1)}, bf16[1,128,1280]{2,1,0:T(8,128)(2,1)}, bf16[1,128,1280]{2,1,0:T(8,128)(2,1)}, f32[8,128]{1,0:T(8,128)}) custom-call(bf16[1,128,1280]{2,1,0:T(8,128)(2,1)} %q_in.1, bf16[1,128,1280]{2,1,0:T(8,128)(2,1)} %k_in.1, bf16[1,128,1280]{2,1,0:T(8,128)(2,1)} %v_in.1, ...), custom_call_target="tpu_custom_call" | custom-call | tf_op jit(solution)/shard_map/attention_block/pallas_call | solution.py:614
  73.7 1.3 %slice_bitcast_fusion = (f32[64]{0:T(128)}, f32[64]{0:T(128)}) fusion(f32[8,128]{1,0:T(8,128)} %get-tuple-element.15), kind=kLoop, calls=%fused_computation | loop fusion | bytes 1024 | tf_op jit(solution)/shard_map/squeeze | solution.py:682
  75.0 0.0 copy-start.2
  75.0 1.8 %copy.17 = bf16[1,128,1280]{2,1,0:T(8,128)(2,1)} copy(bf16[1,128,1280]{2,1,0:T(8,128)(2,1)} %get-tuple-element.24) | data formatting | bytes 655360
  76.8 0.0 copy-done.2
  76.8 0.0 copy-start.1
  76.8 0.7 copy.18
  77.5 0.4 copy-done.1
  77.9 0.0 copy-start
  77.9 0.7 copy.19
  78.6 0.4 copy-done
  78.9 0.7 copy.20
Async XLA Ops:
  75.0 1.8 %copy-start.2 = (bf16[1,128,1280]{2,1,0:T(8,128)(2,1)S(1)}, bf16[1,128,1280]{2,1,0:T(8,128)(2,1)}, u32[]{:S(2)}) copy-start(bf16[1,128,1280]{2,1,0:T(8,128)(2,1)} %get-tuple-element.25) | copy-start | bytes 983044
  76.8 1.1 %copy-start.1 = (bf16[1,128,1280]{2,1,0:T(8,128)(2,1)S(1)}, bf16[1,128,1280]{2,1,0:T(8,128)(2,1)}, u32[]{:S(2)}) copy-start(bf16[1,128,1280]{2,1,0:T(8,128)(2,1)} %get-tuple-element.26) | copy-start | bytes 983044
  77.9 1.1 %copy-start = (bf16[1,128,1280]{2,1,0:T(8,128)(2,1)S(1)}, bf16[1,128,1280]{2,1,0:T(8,128)(2,1)}, u32[]{:S(2)}) copy-start(bf16[1,128,1280]{2,1,0:T(8,128)(2,1)} %get-tuple-element.27) | copy-start | bytes 983044

commit v3 on v2

--- a/solution.py
+++ b/solution.py
@@ -35,11 +35,11 @@
 
 def kernel(
     ny,
-    q_in,
-    k_in,
-    v_in,
+    q_hbm,
+    k_hbm,
+    v_hbm,
     unmerge_in,
-    g_in,
+    g_hbm,
     q_gain,
     k_gain,
     att_out,
@@ -74,7 +74,6 @@
     cell_stage,
     cell_recv,
     gain_own,
-    gain_core,
     gain_x,
     gain_y,
     gain_z,
@@ -94,6 +93,11 @@
     sem_rdr,
     sem_gs,
     sem_gr,
+    sem_in,
+    q_in,
+    k_in,
+    v_in,
+    g_in,
 ):
     img = lax.axis_index("img")
     seq = lax.axis_index("seq")
@@ -112,7 +116,8 @@
     z_peers = [at((z + d) % NZ, x, core) for d in range(1, NZ)]
     y_peers = [((img + d) % ny, seq) for d in range(1, ny)]
     barrier = pltpu.get_barrier_semaphore()
-    greeted = [partner] + x_peers + z_peers + y_peers
+    plane_peers = [partner] + [at(z, (x + d) % NX, c) for d in range(1, NX) for c in (core, other)]
+    greeted = plane_peers + z_peers + y_peers
     for device in greeted:
         pl.semaphore_signal(barrier, inc=1, device_id=device, device_id_type=pl.DeviceIdType.MESH)
 
@@ -126,6 +131,12 @@
             device_id_type=pl.DeviceIdType.MESH,
         )
 
+    loads = [
+        pltpu.make_async_copy(src, dst, sem_in.at[i])
+        for i, (src, dst) in enumerate(((k_hbm, k_in), (v_hbm, v_in), (q_hbm, q_in), (g_hbm, g_in)))
+    ]
+    for load in loads:
+        load.start()
     lane = lax.broadcasted_iota(jnp.int32, (1, 128), 1)
     low = lane < 64
     head_sum = (
@@ -147,6 +158,8 @@
             return jnp.where(low, first, pltpu.roll(second, 64, 1)).astype(BF)
         return jnp.where(low, pltpu.roll(first, 64, 1), second).astype(BF)
 
+    loads[0].wait()
+    loads[1].wait()
     for pair in range(10):
         lanes = slice(pair * 128, pair * 128 + 128)
         raw = k_in[0, :, lanes].astype(F32)
@@ -163,30 +176,8 @@
         else:
             for which in range(2):
                 kv_stage[(pair - 8) * 2 + which, 4] = pick(merged_k, merged_v, which)
-    pl.semaphore_wait(barrier, len(greeted))
-
-    def kv_x(d):
-        return remote(
-            kv_stage.at[(x + d) % NX],
-            kv.at[:, z, core, pl.ds(pl.multiple_of(x * 32, 32), 32), :],
-            sem_xs.at[0, d - 1],
-            sem_xr.at[0, d - 1],
-            x_peers[d - 1],
-        )
-
-    def qg_x(part, d):
-        blocks = pl.ds(0, 3) if part == 0 else pl.ds(3, 2)
-        return remote(
-            qg_stage.at[(x + d) % NX, blocks],
-            qg.at[x, blocks],
-            sem_xs.at[1 + part, d - 1],
-            sem_xr.at[1 + part, d - 1],
-            x_peers[d - 1],
-        )
-
-    for d in range(1, NX):
-        kv_x(d).start()
-    kv[:, z, core, pl.ds(pl.multiple_of(x * 32, 32), 32), :] = kv_stage[x]
+    loads[2].wait()
+    loads[3].wait()
     for pair in range(10):
         lanes = slice(pair * 128, pair * 128 + 128)
         raw = q_in[0, :, lanes].astype(F32)
@@ -201,12 +192,32 @@
             upstream = g_in[0, :, lanes].astype(F32)
             for which in range(2):
                 qg_stage[(pair - 8) * 2 + which, 2] = pick(normed, upstream, which)
-    for d in range(1, NX):
-        qg_x(0, d).start()
     for pair in range(8):
         qg_stage[pair // 2, 3 + pair % 2] = g_in[0, :, pair * 128 : pair * 128 + 128]
-    for d in range(1, NX):
-        qg_x(1, d).start()
+    def kv_x(d):
+        return remote(
+            kv_stage.at[(x + d) % NX],
+            kv.at[:, z, core, pl.ds(pl.multiple_of(x * 32, 32), 32), :],
+            sem_xs.at[0, d - 1],
+            sem_xr.at[0, d - 1],
+            x_peers[d - 1],
+        )
+
+    def qg_x(part, d):
+        blocks = pl.ds(0, 3) if part == 0 else pl.ds(3, 2)
+        return remote(
+            qg_stage.at[(x + d) % NX, blocks],
+            qg.at[x, blocks],
+            sem_xs.at[1 + part, d - 1],
+            sem_xr.at[1 + part, d - 1],
+            x_peers[d - 1],
+        )
+
+    pl.semaphore_wait(barrier, len(greeted))
+
+    for d in range(1, NX):
+        kv_x(d).start()
+    kv[:, z, core, pl.ds(pl.multiple_of(x * 32, 32), 32), :] = kv_stage[x]
     qg[x] = qg_stage[x]
 
     def z_slot(offset):
@@ -250,6 +261,8 @@
     for part in range(2):
         ag_up(1, part).start()
         ag_down(1, part).start()
+    for d in range(1, NX):
+        qg_x(0, d).start()
     for part in range(2):
         ag_partner(0, 0, part).start()
 
@@ -303,6 +316,8 @@
         qm[h] = jnp.where(low == (q_lane < 64), rows, jnp.zeros_like(rows))
         if h == 1:
             gather_hop(2, 0)
+            for d in range(1, NX):
+                qg_x(1, d).start()
     wait_partner((0, 1))
     forward_pair(1, 0, 2)
     gather_hop(2, 1)
@@ -312,12 +327,13 @@
     forward_pair(2, 0, 2)
     gather_hop(3, 1)
     forward_pair(2, 2, 5)
-    gather_hop(4, 0)
-    gather_hop(4, 1)
     for h, (q_block, g_block, q_lane, g_lane) in enumerate(HEADS):
         q_t[h] = jnp.transpose(qm[h].astype(F32))[q_lane : q_lane + 64].astype(BF)
     wait_partner((4, 5))
-    forward_pair(3, 0, 5)
+    forward_pair(3, 0, 2)
+    gather_hop(4, 0)
+    forward_pair(3, 2, 5)
+    gather_hop(4, 1)
     wait_partner((6, 7))
     forward_pair(4, 0, 5)
     for d in range(1, NX):
@@ -460,18 +476,8 @@
             for d in range(1, NX):
                 out_x(1, d).start()
         backward_half(step, 1)
-        reduce_half(step, 0)
-
-    out_stage[:, 3] = jnp.where(low, gq_acc[2], gq_acc[3]).astype(BF).reshape(4, 128, 128)
-    out_stage[:, 4] = (
-        jnp.where(low, gq_acc[4], out_stage[:, 4].reshape(512, 128).astype(F32))
-        .astype(BF)
-        .reshape(4, 128, 128)
-    )
-    for d in range(1, NX):
-        out_x(2, d).start()
-    out_recv[x] = out_stage[x]
-    reduce_half(3, 1)
+        if step < 3:
+            reduce_half(step, 0)
 
     def gain_copies(stage):
         base, buffer, mine, peers = gain_stages[stage]
@@ -497,15 +503,26 @@
         return result
 
     gain_stages = (
-        (0, gain_core, core, [partner]),
-        (1, gain_x, x, x_peers),
-        (4, gain_y, img, y_peers),
+        (0, gain_x, x * 2 + core, plane_peers),
         (7, gain_z, z, z_peers),
+        (14, gain_y, img, y_peers),
     )
     tile = jnp.zeros((8, 128), F32)
     for h in range(5):
         tile = tile + jnp.sum((qm[h].astype(F32) * gq_acc[h]).reshape(64, 8, 128), axis=0)
     gain_send(0, tile)
+    reduce_half(3, 0)
+
+    out_stage[:, 3] = jnp.where(low, gq_acc[2], gq_acc[3]).astype(BF).reshape(4, 128, 128)
+    out_stage[:, 4] = (
+        jnp.where(low, gq_acc[4], out_stage[:, 4].reshape(512, 128).astype(F32))
+        .astype(BF)
+        .reshape(4, 128, 128)
+    )
+    for d in range(1, NX):
+        out_x(2, d).start()
+    out_recv[x] = out_stage[x]
+    reduce_half(3, 1)
 
     def join(first, second, which):
         if which == 0:
@@ -558,8 +575,6 @@
         unit = q_unit[:, lanes]
         inner = head_mean(grad * unit)
         gq_out[0, :, lanes] = (q_scale[:, lanes] * (grad - unit * inner)).astype(BF)
-        if pair == 4:
-            gain_send(3, gain_sum(2))
 
     for d in range(1, NX):
         cell_x(d).wait_recv()
@@ -579,7 +594,7 @@
         inner = head_mean(grad * unit)
         gk_out[0, :, lanes] = (k_scale[:, lanes] * (grad - unit * inner)).astype(BF)
 
-    row = jnp.sum(gain_sum(3), axis=0, keepdims=True)
+    row = jnp.sum(gain_sum(2), axis=0, keepdims=True)
     row = row + pltpu.roll(row, 64, 1)
     gain_out[...] = jnp.broadcast_to(row / jnp.where(low, gain_q, gain_k), (8, 128))
 
@@ -602,9 +617,18 @@
             ag_partner(i, 0, part).wait_send()
         for step in range(4):
             core_copy(step, part).wait_send()
-    for stage in range(4):
+    for stage in range(3):
         for copy in gain_copies(stage):
             copy.wait_send()
+
+
+def finish(att, gq, gk, gv, gain, att_out, gq_out, gk_out, gv_out, q_gain_out, k_gain_out):
+    att_out[...] = att[...]
+    gq_out[...] = gq[...]
+    gk_out[...] = gk[...]
+    gv_out[...] = gv[...]
+    q_gain_out[...] = gain[0:1, :64]
+    k_gain_out[...] = pltpu.roll(gain[...], 64, 1)[0:1, :64]
 
 
 def local(ny, query_proj, key_proj, value_proj, merge_cells, unmerge, grad_out, query_gain, key_gain):
@@ -615,7 +639,9 @@
         functools.partial(kernel, ny),
         out_shape=[jax.ShapeDtypeStruct((1, 128, 1280), BF)] * 4
         + [jax.ShapeDtypeStruct((8, 128), F32)],
-        in_specs=[pl.BlockSpec(memory_space=pltpu.VMEM)] * 7,
+        in_specs=[pl.BlockSpec(memory_space=pl.ANY)] * 3
+        + [pl.BlockSpec(memory_space=pltpu.VMEM), pl.BlockSpec(memory_space=pl.ANY)]
+        + [pl.BlockSpec(memory_space=pltpu.VMEM)] * 2,
         out_specs=[pl.BlockSpec(memory_space=pltpu.VMEM)] * 5,
         scratch_shapes=[
             vmem((128, 1280), F32),
@@ -645,8 +671,7 @@
             vmem(block, BF),
             vmem((4, 5, 32, 128), BF),
             vmem((4, 8, 128), F32),
-            vmem((2, 8, 128), F32),
-            vmem((NX, 8, 128), F32),
+            vmem((2 * NX, 8, 128), F32),
             vmem((ny, 8, 128), F32),
             vmem((NZ, 8, 128), F32),
             dma((7, 3)),
@@ -663,8 +688,13 @@
             dma((4, 2)),
             dma((4, 2)),
             dma((4, 2)),
-            dma((14,)),
-            dma((14,)),
+            dma((17,)),
+            dma((17,)),
+            dma((4,)),
+            vmem((1, 128, 1280), BF),
+            vmem((1, 128, 1280), BF),
+            vmem((1, 128, 1280), BF),
+            vmem((1, 128, 1280), BF),
         ],
         compiler_params=pltpu.CompilerParams(
             collective_id=0, has_side_effects=True, vmem_limit_bytes=60 * 1024 * 1024
@@ -679,7 +709,14 @@
         query_gain.reshape(1, 64),
         key_gain.reshape(1, 64),
     )
-    return (outs[0], outs[1], outs[2], outs[3], outs[4][0, :64], outs[4][0, 64:])
+    done = pl.pallas_call(
+        finish,
+        out_shape=[jax.ShapeDtypeStruct((1, 128, 1280), BF)] * 4 + [jax.ShapeDtypeStruct((1, 64), F32)] * 2,
+        in_specs=[pl.BlockSpec(memory_space=pltpu.VMEM)] * 5,
+        out_specs=[pl.BlockSpec(memory_space=pltpu.VMEM)] * 6,
+        name="finish",
+    )(*outs)
+    return (*done[:4], done[4].reshape(64), done[5].reshape(64))
 
 
 def solution(mesh):

time: 79.9 us -> 70.5 us (0.88)
  local copies, waits for them, and re-layouts: 6.01 us -> 0 us
  Pallas kernels: 73 us -> 68.9 us
    pallas_call x1, Pallas kernels: 73 us -> 66.6 us  [local(): pl.pallas_call(functools.partial(kernel, ny), out_shape=[jax.ShapeDtypeSt...]
    unnamed x10 -> x0, local copies, waits for them, and re-layouts: 4.67 us -> none
    pallas_call x0 -> x1, Pallas kernels: none -> 2.35 us  [local(): pl.pallas_call(finish, out_shape=[jax.ShapeDtypeStruct((1, 128, 1280), BF...]
    squeeze x1 -> x0, local copies, waits for them, and re-layouts: 1.34 us -> none  [local(): outs[4][0, 64:]]
where the time goes in v3:
time: 70.5 us; the launch traced here: 69.5 us
  Pallas kernels  68.9 us (98%)
    pallas_call x1, Pallas kernels, local(): pl.pallas_call(functools.partial(kernel, ny), out_shape=[jax.ShapeDtypeSt...  66.6 us
    pallas_call x1, Pallas kernels, local(): pl.pallas_call(finish, out_shape=[jax.ShapeDtypeStruct((1, 128, 1280), BF...  2.35 us

profile of v3, /device:TPU:1, one launch (start us, length us, event | category | flops | bytes accessed | tf_op | source)
XLA Modules:
  0.0 69.5 jit_solution(2847422550515505562)
XLA Ops:
  0.6 66.6 %attention_block.1 = (bf16[1,128,1280]{2,1,0:T(8,128)(2,1)}, bf16[1,128,1280]{2,1,0:T(8,128)(2,1)}, bf16[1,128,1280]{2,1,0:T(8,128)(2,1)}, bf16[1,128,1280]{2,1,0:T(8,128)(2,1)}, f32[8,128]{1,0:T(8,128)}) custom-call(bf16[1,128,1280]{2,1,0:T(8,128)(2,1)} %q_hbm.1, bf16[1,128,1280]{2,1,0:T(8,128)(2,1)} %k_hbm.1, bf16[1,128,1280]{2,1,0:T(8,128)(2,1)} %v_hbm.1, ...), custom_call_target="tpu_custom_call" | custom-call | tf_op jit(solution)/shard_map/attention_block/pallas_call | solution.py:638
  67.2 2.3 %finish.1 = (bf16[1,128,1280]{2,1,0:T(8,128)(2,1)}, bf16[1,128,1280]{2,1,0:T(8,128)(2,1)}, bf16[1,128,1280]{2,1,0:T(8,128)(2,1)}, bf16[1,128,1280]{2,1,0:T(8,128...) custom-call(bf16[1,128,1280]{2,1,0:T(8,128)(2,1)} %get-tuple-element.17.att, bf16[1,128,1280]{2,1,0:T(8,128)(2,1)} %get-tuple-element.18.gq, ...), custom_call_target="tpu_custom_call" | custom-call | tf_op jit(solution)/shard_map/finish/pallas_call | solution.py:712

commit v4 on v3

--- a/solution.py
+++ b/solution.py
@@ -13,7 +13,8 @@
 NZ, NX = 8, 4
 HEADS = ((0, 1, 0, 0), (0, 1, 64, 64), (2, 3, 0, 0), (2, 3, 64, 64), (4, 4, 0, 64))
 Q_AT = {0: 0, 2: 1, 4: 2, 1: 3, 3: 4}
-PARTS = ((0, 2), (2, 3))
+PARTS = ((0, 2), (2, 2), (4, 1))
+PART_HEADS = ((0, 2), (2, 4), (4, 5))
 
 
 def dot(a, b):
@@ -75,7 +76,6 @@
     cell_recv,
     gain_own,
     gain_x,
-    gain_y,
     gain_z,
     sem_xs,
     sem_xr,
@@ -93,6 +93,8 @@
     sem_rdr,
     sem_gs,
     sem_gr,
+    sem_fs,
+    sem_fr,
     sem_in,
     q_in,
     k_in,
@@ -109,15 +111,20 @@
     def at(zz, xx, cc):
         return (img, (zz * NX + xx) * 2 + cc)
 
+    sign = 1 - 2 * core
+    onward = at((z + sign + NZ) % NZ, x, core)
     up = at((z + 1) % NZ, x, core)
     down = at((z + NZ - 1) % NZ, x, core)
     partner = at(z, x, other)
     x_peers = [at(z, (x + d) % NX, core) for d in range(1, NX)]
     z_peers = [at((z + d) % NZ, x, core) for d in range(1, NZ)]
-    y_peers = [((img + d) % ny, seq) for d in range(1, ny)]
     barrier = pltpu.get_barrier_semaphore()
     plane_peers = [partner] + [at(z, (x + d) % NX, c) for d in range(1, NX) for c in (core, other)]
-    greeted = plane_peers + z_peers + y_peers
+    for e in range(1, ny):
+        for d in range(NX):
+            for c in (core, other):
+                plane_peers.append(((img + e) % ny, (z * NX + (x + d) % NX) * 2 + c))
+    greeted = plane_peers + z_peers
     for device in greeted:
         pl.semaphore_signal(barrier, inc=1, device_id=device, device_id_type=pl.DeviceIdType.MESH)
 
@@ -135,8 +142,8 @@
         pltpu.make_async_copy(src, dst, sem_in.at[i])
         for i, (src, dst) in enumerate(((k_hbm, k_in), (v_hbm, v_in), (q_hbm, q_in), (g_hbm, g_in)))
     ]
-    for load in loads:
-        load.start()
+    loads[0].start()
+    loads[1].start()
     lane = lax.broadcasted_iota(jnp.int32, (1, 128), 1)
     low = lane < 64
     head_sum = (
@@ -144,9 +151,10 @@
         == (lax.broadcasted_iota(jnp.int32, (128, 128), 1) < 64)
     ).astype(F32).astype(BF)
 
+    head_sum2 = jnp.concatenate([head_sum, head_sum], axis=0)
+
     def head_mean(value):
-        high, rest = split(value)
-        return (dot(high, head_sum) + dot(rest, head_sum)) * (1.0 / 64.0)
+        return dot(jnp.concatenate(split(value), axis=1), head_sum2) * (1.0 / 64.0)
 
     gain_q = jnp.concatenate([q_gain[...], q_gain[...]], axis=1)
     gain_k = jnp.concatenate([k_gain[...], k_gain[...]], axis=1)
@@ -158,24 +166,34 @@
             return jnp.where(low, first, pltpu.roll(second, 64, 1)).astype(BF)
         return jnp.where(low, pltpu.roll(first, 64, 1), second).astype(BF)
 
+    member2 = jnp.concatenate([member, member], axis=1)
     loads[0].wait()
+    loads[2].start()
+    loads[3].start()
+    merged_k = []
+    for two in range(5):
+        normed = []
+        for pair in (2 * two, 2 * two + 1):
+            lanes = slice(pair * 128, pair * 128 + 128)
+            raw = k_in[0, :, lanes].astype(F32)
+            scale = lax.rsqrt(head_mean(raw * raw) + EPSILON)
+            unit = raw * scale
+            k_unit[:, lanes] = unit
+            k_scale[:, lanes] = scale
+            normed.append(unit * gain_k)
+        rows = jnp.concatenate(split(jnp.concatenate(normed, axis=1)), axis=0)
+        merged_k.append(dot(member2, rows) * 0.25)
     loads[1].wait()
-    for pair in range(10):
-        lanes = slice(pair * 128, pair * 128 + 128)
-        raw = k_in[0, :, lanes].astype(F32)
-        scale = lax.rsqrt(head_mean(raw * raw) + EPSILON)
-        unit = raw * scale
-        k_unit[:, lanes] = unit
-        k_scale[:, lanes] = scale
-        high, rest = split(unit * gain_k)
-        merged_k = (dot(member, high) + dot(member, rest)) * 0.25
-        merged_v = dot(member, v_in[0, :, lanes]) * 0.25
-        if pair < 8:
-            kv_stage[pair // 2, (pair % 2) * 2] = merged_k.astype(BF)
-            kv_stage[pair // 2, (pair % 2) * 2 + 1] = merged_v.astype(BF)
-        else:
-            for which in range(2):
-                kv_stage[(pair - 8) * 2 + which, 4] = pick(merged_k, merged_v, which)
+    for two in range(5):
+        merged_v = dot(member, v_in[0, :, two * 256 : two * 256 + 256]) * 0.25
+        for i in range(2):
+            one_k, one_v = merged_k[two][:, i * 128 : i * 128 + 128], merged_v[:, i * 128 : i * 128 + 128]
+            if two < 4:
+                kv_stage[two, 2 * i] = one_k.astype(BF)
+                kv_stage[two, 2 * i + 1] = one_v.astype(BF)
+            else:
+                for which in range(2):
+                    kv_stage[2 * i + which, 4] = pick(one_k, one_v, which)
     loads[2].wait()
     loads[3].wait()
     for pair in range(10):
@@ -226,45 +244,51 @@
     def blocks_of(part):
         return pl.ds(*PARTS[part])
 
-    def ag_up(s, part):
-        ref = kv.at[blocks_of(part), z_slot(1 - s), core]
-        return remote(ref, ref, sem_us.at[s - 1, part], sem_ur.at[s - 1, part], up)
-
-    def ag_down(s, part):
-        ref = kv.at[blocks_of(part), z_slot(s - 1), core]
-        return remote(ref, ref, sem_ds.at[s - 1, part], sem_dr.at[s - 1, part], down)
-
-    def ag_partner(i, offset, part):
-        ref = kv.at[blocks_of(part), z_slot(offset), core]
-        return remote(ref, ref, sem_ps.at[i, part], sem_pr.at[i, part], partner)
-
-    def on_up(s, part):
-        return s < 4 or part == 0
-
-    def on_down(s, part):
-        return s < 4 or part == 1
+    def far(s):
+        return z_slot(-sign * s)
+
+    def half(part):
+        return core if part == 0 else other
+
+    def ag_ring(s, part):
+        ref = kv.at[:, far(s - 1), half(part)]
+        return remote(ref, ref, sem_us.at[s - 1, part], sem_ur.at[s - 1, part], onward)
+
+    def ag_partner(s, part):
+        ref = kv.at[:, far(s), half(part)]
+        return remote(ref, ref, sem_ps.at[s, part], sem_pr.at[s, part], partner)
+
+    def piece(index, d):
+        return kv.at[:, z, index, pl.ds(pl.multiple_of(((x + NX - d) % NX) * 32, 32), 32), :]
+
+    def first_ring(part, d):
+        ref = piece(half(part), d)
+        return remote(ref, ref, sem_fs.at[part, d], sem_fr.at[part, d], onward)
+
+    def first_partner(d):
+        ref = piece(core, d)
+        return remote(ref, ref, sem_fs.at[2, d], sem_fr.at[2, d], partner)
 
     def gather_hop(s, part):
-        if on_up(s, part):
-            ag_up(s, part).wait_recv()
-            if s < 4 and on_up(s + 1, part):
-                ag_up(s + 1, part).start()
-            ag_partner(2 * s - 1, -s, part).start()
-        if on_down(s, part):
-            ag_down(s, part).wait_recv()
-            if s < 4 and on_down(s + 1, part):
-                ag_down(s + 1, part).start()
-            ag_partner(2 * s if s < 4 else 7, s, part).start()
-
-    for d in range(1, NX):
-        kv_x(d).wait_recv()
-    for part in range(2):
-        ag_up(1, part).start()
-        ag_down(1, part).start()
+        if s == 1:
+            for d in range(NX):
+                first_ring(part, d).wait_recv()
+        else:
+            ag_ring(s, part).wait_recv()
+        if s < 3 or (s == 3 and part == 0):
+            ag_ring(s + 1, part).start()
+        ag_partner(s, part).start()
+
+    for d in (0, 1, 3, 2):
+        if d > 0:
+            kv_x(d).wait_recv()
+        first_ring(0, d).start()
+        first_partner(d).start()
     for d in range(1, NX):
         qg_x(0, d).start()
-    for part in range(2):
-        ag_partner(0, 0, part).start()
+    for d in (0, 1, 3, 2):
+        first_partner(d).wait_recv()
+        first_ring(1, d).start()
 
     def head_blocks(h):
         single = (h == 4).astype(jnp.int32)
@@ -298,12 +322,11 @@
         lax.fori_loop(start, stop, body, 0)
 
     def forward_pair(s, start, stop):
-        forward(z_slot(-s), z_slot(s - 1), start, stop)
-
-    def wait_partner(indices):
-        for i in indices:
-            for part in range(2):
-                ag_partner(i, 0, part).wait_recv()
+        forward(far(s), far(1 - s), start, stop)
+
+    def wait_partner(s):
+        for part in range(2 if s < 4 else 1):
+            ag_partner(s, part).wait_recv()
 
     acc[...] = jnp.zeros_like(acc)
     gq_acc[...] = jnp.zeros_like(gq_acc)
@@ -318,29 +341,24 @@
             gather_hop(2, 0)
             for d in range(1, NX):
                 qg_x(1, d).start()
-    wait_partner((0, 1))
     forward_pair(1, 0, 2)
     gather_hop(2, 1)
     forward_pair(1, 2, 5)
     gather_hop(3, 0)
-    wait_partner((2, 3))
+    wait_partner(1)
     forward_pair(2, 0, 2)
     gather_hop(3, 1)
     forward_pair(2, 2, 5)
     for h, (q_block, g_block, q_lane, g_lane) in enumerate(HEADS):
         q_t[h] = jnp.transpose(qm[h].astype(F32))[q_lane : q_lane + 64].astype(BF)
-    wait_partner((4, 5))
+    wait_partner(2)
     forward_pair(3, 0, 2)
     gather_hop(4, 0)
     forward_pair(3, 2, 5)
-    gather_hop(4, 1)
-    wait_partner((6, 7))
-    forward_pair(4, 0, 5)
-    for d in range(1, NX):
-        qg_x(1, d).wait_recv()
-
-    attended = []
-    for h, (q_block, g_block, q_lane, g_lane) in enumerate(HEADS):
+    wait_partner(3)
+    wait_partner(4)
+    def finish_head(h):
+        q_block, g_block, q_lane, g_lane = HEADS[h]
         mine = low == (g_lane < 64)
         total = acc[h]
         inverse = pltpu.roll(1.0 / total, 64, 1)
@@ -355,12 +373,17 @@
             jnp.where(lane == spare, -high, jnp.where(lane == spare + 1, -rest, jnp.zeros_like(scaled))),
         )
         g_t[h] = jnp.transpose(scaled.astype(F32))[g_lane : g_lane + 64].astype(BF)
-        if h == 0 or h == 2:
-            held = weighted
-        elif h == 4:
-            out_stage[:, 4] = weighted.reshape(4, 128, 128)
+        return weighted
+
+    def finalize(part):
+        if part == 0:
+            pairs = (0,)
         else:
-            out_stage[:, h // 2] = jnp.where(low, held, weighted).reshape(4, 128, 128)
+            pairs = (1,)
+            out_stage[:, 4] = finish_head(4).reshape(4, 128, 128)
+        for pair in pairs:
+            first, second = finish_head(2 * pair), finish_head(2 * pair + 1)
+            out_stage[:, pair] = jnp.where(low, first, second).reshape(4, 128, 128)
 
     def out_x(part, d):
         blocks = pl.ds(*((0, 2), (2, 1), (3, 2))[part])
@@ -371,9 +394,6 @@
             sem_xr.at[3 + part, d - 1],
             x_peers[d - 1],
         )
-
-    for d in range(1, NX):
-        out_x(0, d).start()
 
     def backward(step, first, second, start, stop):
         def body(h, carry):
@@ -423,7 +443,7 @@
     def send_up(hop, step, i, part):
         value = chip_sum(step, i, part)
         blocks = blocks_of(part)
-        if hop > 0 and not (hop == 1 and part == 1):
+        if hop > 0 and not (hop == 1 and part > 0):
             rs_up(hop - 1, part).wait_recv()
             value = value + up_recv[hop - 1, blocks].astype(F32)
         up_send[hop, blocks] = value.astype(BF)
@@ -443,8 +463,8 @@
         if step == 0 and part == 0:
             send_up(0, 0, 0, 0)
         elif step == 0:
-            send_down(0, 0, 0, 1)
-            send_up(1, 0, 1, 1)
+            send_down(0, 0, 0, part)
+            send_up(1, 0, 1, part)
         elif step == 1 and part == 0:
             send_down(1, 1, 0, 0)
             send_up(1, 0, 1, 0)
@@ -452,8 +472,8 @@
             if step == 2 and part == 0:
                 send_up(2, 1, 1, 0)
             send_down(step, step, 0, part)
-            if part == 1:
-                send_up(step + 1, step, 1, 1)
+            if part > 0:
+                send_up(step + 1, step, 1, part)
         else:
             if part == 0:
                 send_up(3, 2, 1, 0)
@@ -462,22 +482,43 @@
     def backward_half(step, part):
         first = z_slot((4, -3, -2, -1)[step])
         second = z_slot((3, 2, 1, 0)[step])
-        backward(step, first, second, *((0, 2), (2, 5))[part])
+        backward(step, first, second, *PART_HEADS[part])
         blocks = blocks_of(part)
         core_send[step, :, blocks] = g_all[step, :, other, blocks].astype(BF)
         core_copy(step, part).start()
 
-    for step in range(4):
-        backward_half(step, 0)
-        if step > 0:
-            reduce_half(step - 1, 1)
-        if step == 3:
-            out_stage[:, 2] = jnp.where(low, gq_acc[0], gq_acc[1]).astype(BF).reshape(4, 128, 128)
-            for d in range(1, NX):
-                out_x(1, d).start()
-        backward_half(step, 1)
-        if step < 3:
-            reduce_half(step, 0)
+    forward_pair(4, 0, 2)
+    for d in range(1, NX):
+        qg_x(1, d).wait_recv()
+    finalize(0)
+    backward_half(0, 0)
+    forward_pair(4, 2, 5)
+    finalize(1)
+    for d in range(1, NX):
+        out_x(0, d).start()
+    reduce_half(0, 0)
+    backward_half(0, 1)
+    backward_half(0, 2)
+    backward_half(1, 0)
+    reduce_half(0, 1)
+    reduce_half(0, 2)
+    backward_half(1, 1)
+    backward_half(1, 2)
+    reduce_half(1, 0)
+    backward_half(2, 0)
+    reduce_half(1, 1)
+    reduce_half(1, 2)
+    backward_half(2, 1)
+    backward_half(2, 2)
+    reduce_half(2, 0)
+    backward_half(3, 0)
+    out_stage[:, 2] = jnp.where(low, gq_acc[0], gq_acc[1]).astype(BF).reshape(4, 128, 128)
+    for d in range(1, NX):
+        out_x(1, d).start()
+    reduce_half(2, 1)
+    reduce_half(2, 2)
+    backward_half(3, 1)
+    backward_half(3, 2)
 
     def gain_copies(stage):
         base, buffer, mine, peers = gain_stages[stage]
@@ -503,14 +544,13 @@
         return result
 
     gain_stages = (
-        (0, gain_x, x * 2 + core, plane_peers),
-        (7, gain_z, z, z_peers),
-        (14, gain_y, img, y_peers),
+        (0, gain_x, (img * NX + x) * 2 + core, plane_peers),
+        (len(plane_peers), gain_z, z, z_peers),
     )
     tile = jnp.zeros((8, 128), F32)
     for h in range(5):
         tile = tile + jnp.sum((qm[h].astype(F32) * gq_acc[h]).reshape(64, 8, 128), axis=0)
-    gain_send(0, tile)
+    gain_send(0, jnp.sum(tile, axis=0, keepdims=True))
     reduce_half(3, 0)
 
     out_stage[:, 3] = jnp.where(low, gq_acc[2], gq_acc[3]).astype(BF).reshape(4, 128, 128)
@@ -523,6 +563,7 @@
         out_x(2, d).start()
     out_recv[x] = out_stage[x]
     reduce_half(3, 1)
+    reduce_half(3, 2)
 
     def join(first, second, which):
         if which == 0:
@@ -530,7 +571,7 @@
         return jnp.where(low, pltpu.roll(first, 64, 1), second)
 
     def final_sum():
-        for part in range(2):
+        for part in range(3):
             rs_up(3, part).wait_recv()
             rs_down(3, part).wait_recv()
         for b in range(5):
@@ -552,12 +593,11 @@
         out_x(0, d).wait_recv()
     for pair in range(8):
         att_out[0, :, pair * 128 : pair * 128 + 128] = out_recv[pair // 2, pair % 2]
-    gain_send(1, gain_sum(0))
     final_sum()
     for d in range(1, NX):
         cell_x(d).start()
     cell_recv[x] = cell_stage[:, pl.ds(pl.multiple_of(x * 32, 32), 32), :]
-    gain_send(2, gain_sum(1))
+    gain_send(1, gain_sum(0))
 
     for part in (1, 2):
         for d in range(1, NX):
@@ -594,7 +634,7 @@
         inner = head_mean(grad * unit)
         gk_out[0, :, lanes] = (k_scale[:, lanes] * (grad - unit * inner)).astype(BF)
 
-    row = jnp.sum(gain_sum(2), axis=0, keepdims=True)
+    row = gain_sum(1)
     row = row + pltpu.roll(row, 64, 1)
     gain_out[...] = jnp.broadcast_to(row / jnp.where(low, gain_q, gain_k), (8, 128))
 
@@ -605,19 +645,24 @@
         for part in range(3):
             out_x(part, d).wait_send()
         cell_x(d).wait_send()
-    for part in range(2):
-        for s in range(1, 5):
-            if on_up(s, part):
-                ag_up(s, part).wait_send()
-                rs_up(4 - s, part).wait_send()
-            if on_down(s, part):
-                ag_down(s, part).wait_send()
-                rs_down(4 - s, part).wait_send()
-        for i in range(8):
-            ag_partner(i, 0, part).wait_send()
-        for step in range(4):
+    for d in range(NX):
+        first_partner(d).wait_send()
+        for part in range(2):
+            first_ring(part, d).wait_send()
+    for s in range(1, 5):
+        for part in range(2):
+            if s < 4 or part == 0:
+                if s > 1:
+                    ag_ring(s, part).wait_send()
+                ag_partner(s, part).wait_send()
+    for step in range(4):
+        for part in range(3):
             core_copy(step, part).wait_send()
-    for stage in range(3):
+            if step > 0 or part == 0:
+                rs_up(step, part).wait_send()
+            if step > 0 or part > 0:
+                rs_down(step, part).wait_send()
+    for stage in range(2):
         for copy in gain_copies(stage):
             copy.wait_send()
 
@@ -670,26 +715,27 @@
             vmem((4,) + block, BF),
             vmem(block, BF),
             vmem((4, 5, 32, 128), BF),
-            vmem((4, 8, 128), F32),
-            vmem((2 * NX, 8, 128), F32),
-            vmem((ny, 8, 128), F32),
-            vmem((NZ, 8, 128), F32),
+            vmem((2, 1, 128), F32),
+            vmem((2 * NX * ny, 1, 128), F32),
+            vmem((NZ, 1, 128), F32),
             dma((7, 3)),
             dma((7, 3)),
-            dma((4, 2)),
-            dma((4, 2)),
-            dma((4, 2)),
-            dma((4, 2)),
+            dma((4, 3)),
+            dma((4, 3)),
+            dma((4, 3)),
+            dma((4, 3)),
             dma((8, 2)),
             dma((8, 2)),
-            dma((4, 2)),
-            dma((4, 2)),
-            dma((4, 2)),
-            dma((4, 2)),
-            dma((4, 2)),
-            dma((4, 2)),
-            dma((17,)),
-            dma((17,)),
+            dma((4, 3)),
+            dma((4, 3)),
+            dma((4, 3)),
+            dma((4, 3)),
+            dma((4, 3)),
+            dma((4, 3)),
+            dma((2 * NX * ny - 1 + NZ - 1,)),
+            dma((2 * NX * ny - 1 + NZ - 1,)),
+            dma((3, 4)),
+            dma((3, 4)),
             dma((4,)),
             vmem((1, 128, 1280), BF),
             vmem((1, 128, 1280), BF),

time: 70.5 us -> 67.9 us (0.963); the launches traced: 69.5 us -> 67.7 us
  Pallas kernels: 68.9 us -> 67.1 us
    pallas_call x1, Pallas kernels: 66.6 us -> 64.7 us  [local(): pl.pallas_call(functools.partial(kernel, ny), out_shape=[jax.ShapeDtypeSt...]
where the time goes in v4:
time: 67.9 us; the launch traced here: 67.7 us
  Pallas kernels  67.1 us (99%)
    pallas_call x1, Pallas kernels, local(): pl.pallas_call(functools.partial(kernel, ny), out_shape=[jax.ShapeDtypeSt...  64.7 us
    pallas_call x1, Pallas kernels, local(): pl.pallas_call(finish, out_shape=[jax.ShapeDtypeStruct((1, 128, 1280), BF...  2.35 us

profile of v4, /device:TPU:1, one launch (start us, length us, event | category | flops | bytes accessed | tf_op | source)
XLA Modules:
  0.0 67.7 jit_solution(11181202284797611070)
XLA Ops:
  0.6 64.7 %attention_block.1 = (bf16[1,128,1280]{2,1,0:T(8,128)(2,1)}, bf16[1,128,1280]{2,1,0:T(8,128)(2,1)}, bf16[1,128,1280]{2,1,0:T(8,128)(2,1)}, bf16[1,128,1280]{2,1,0:T(8,128)(2,1)}, f32[8,128]{1,0:T(8,128)}) custom-call(bf16[1,128,1280]{2,1,0:T(8,128)(2,1)} %q_hbm.1, bf16[1,128,1280]{2,1,0:T(8,128)(2,1)} %k_hbm.1, bf16[1,128,1280]{2,1,0:T(8,128)(2,1)} %v_hbm.1, ...), custom_call_target="tpu_custom_call" | custom-call | tf_op jit(solution)/shard_map/attention_block/pallas_call | solution.py:683
  65.4 2.3 %finish.1 = (bf16[1,128,1280]{2,1,0:T(8,128)(2,1)}, bf16[1,128,1280]{2,1,0:T(8,128)(2,1)}, bf16[1,128,1280]{2,1,0:T(8,128)(2,1)}, bf16[1,128,1280]{2,1,0:T(8,128...) custom-call(bf16[1,128,1280]{2,1,0:T(8,128)(2,1)} %get-tuple-element.17.att, bf16[1,128,1280]{2,1,0:T(8,128)(2,1)} %get-tuple-element.18.gq, ...), custom_call_target="tpu_custom_call" | custom-call | tf_op jit(solution)/shard_map/finish/pallas_call | solution.py:758

commit v5 on v4

--- a/solution.py
+++ b/solution.py
@@ -570,32 +570,38 @@
             return jnp.where(low, first, pltpu.roll(second, 64, 1))
         return jnp.where(low, pltpu.roll(first, 64, 1), second)
 
+    def cell_x(part, d):
+        blocks = blocks_of(part)
+        rows = pl.ds(pl.multiple_of(((x + d) % NX) * 32, 32), 32)
+        return remote(
+            cell_stage.at[blocks, rows, :],
+            cell_recv.at[x, blocks],
+            sem_xs.at[6 + part, d - 1],
+            sem_xr.at[6 + part, d - 1],
+            x_peers[d - 1],
+        )
+
     def final_sum():
         for part in range(3):
             rs_up(3, part).wait_recv()
             rs_down(3, part).wait_recv()
-        for b in range(5):
-            total = (
-                g_all[3, 1, core, b]
-                + core_recv[3, 1, b].astype(F32)
-                + up_recv[3, b].astype(F32)
-                + dn_recv[3, b].astype(F32)
-            )
-            cell_stage[b] = jnp.transpose(total).astype(BF)
-
-    def cell_x(d):
-        rows = pl.ds(pl.multiple_of(((x + d) % NX) * 32, 32), 32)
-        return remote(
-            cell_stage.at[:, rows, :], cell_recv.at[x], sem_xs.at[6, d - 1], sem_xr.at[6, d - 1], x_peers[d - 1]
-        )
+            first, count = PARTS[part]
+            for b in range(first, first + count):
+                total = (
+                    g_all[3, 1, core, b]
+                    + core_recv[3, 1, b].astype(F32)
+                    + up_recv[3, b].astype(F32)
+                    + dn_recv[3, b].astype(F32)
+                )
+                cell_stage[b] = jnp.transpose(total).astype(BF)
+            for d in range(1, NX):
+                cell_x(part, d).start()
 
     for d in range(1, NX):
         out_x(0, d).wait_recv()
     for pair in range(8):
         att_out[0, :, pair * 128 : pair * 128 + 128] = out_recv[pair // 2, pair % 2]
     final_sum()
-    for d in range(1, NX):
-        cell_x(d).start()
     cell_recv[x] = cell_stage[:, pl.ds(pl.multiple_of(x * 32, 32), 32), :]
     gain_send(1, gain_sum(0))
 
@@ -616,8 +622,9 @@
         inner = head_mean(grad * unit)
         gq_out[0, :, lanes] = (q_scale[:, lanes] * (grad - unit * inner)).astype(BF)
 
-    for d in range(1, NX):
-        cell_x(d).wait_recv()
+    for part in range(3):
+        for d in range(1, NX):
+            cell_x(part, d).wait_recv()
     for pair in range(10):
         lanes = slice(pair * 128, pair * 128 + 128)
         if pair < 8:
@@ -644,7 +651,8 @@
             qg_x(part, d).wait_send()
         for part in range(3):
             out_x(part, d).wait_send()
-        cell_x(d).wait_send()
+        for part in range(3):
+            cell_x(part, d).wait_send()
     for d in range(NX):
         first_partner(d).wait_send()
         for part in range(2):
@@ -718,8 +726,8 @@
             vmem((2, 1, 128), F32),
             vmem((2 * NX * ny, 1, 128), F32),
             vmem((NZ, 1, 128), F32),
-            dma((7, 3)),
-            dma((7, 3)),
+            dma((9, 3)),
+            dma((9, 3)),
             dma((4, 3)),
             dma((4, 3)),
             dma((4, 3)),

time: 67.9 us -> 68 us (level)
  no operation moved by 1% of the time
where the time goes in v5:
time: 68 us; the launch traced here: 67.8 us
  Pallas kernels  67.2 us (99%)
    pallas_call x1, Pallas kernels, local(): pl.pallas_call(functools.partial(kernel, ny), out_shape=[jax.ShapeDtypeSt...  64.9 us
    pallas_call x1, Pallas kernels, local(): pl.pallas_call(finish, out_shape=[jax.ShapeDtypeStruct((1, 128, 1280), BF...  2.35 us

profile of v5, /device:TPU:1, one launch (start us, length us, event | category | flops | bytes accessed | tf_op | source)
XLA Modules:
  0.0 67.8 jit_solution(10109343442476303253)
XLA Ops:
  0.6 64.9 %attention_block.1 = (bf16[1,128,1280]{2,1,0:T(8,128)(2,1)}, bf16[1,128,1280]{2,1,0:T(8,128)(2,1)}, bf16[1,128,1280]{2,1,0:T(8,128)(2,1)}, bf16[1,128,1280]{2,1,0:T(8,128)(2,1)}, f32[8,128]{1,0:T(8,128)}) custom-call(bf16[1,128,1280]{2,1,0:T(8,128)(2,1)} %q_hbm.1, bf16[1,128,1280]{2,1,0:T(8,128)(2,1)} %k_hbm.1, bf16[1,128,1280]{2,1,0:T(8,128)(2,1)} %v_hbm.1, ...), custom_call_target="tpu_custom_call" | custom-call | tf_op jit(solution)/shard_map/attention_block/pallas_call | solution.py:691
  65.5 2.3 %finish.1 = (bf16[1,128,1280]{2,1,0:T(8,128)(2,1)}, bf16[1,128,1280]{2,1,0:T(8,128)(2,1)}, bf16[1,128,1280]{2,1,0:T(8,128)(2,1)}, bf16[1,128,1280]{2,1,0:T(8,128...) custom-call(bf16[1,128,1280]{2,1,0:T(8,128)(2,1)} %get-tuple-element.17.att, bf16[1,128,1280]{2,1,0:T(8,128)(2,1)} %get-tuple-element.18.gq, ...), custom_call_target="tpu_custom_call" | custom-call | tf_op jit(solution)/shard_map/finish/pallas_call | solution.py:766
